TPU v7x, 128 devices: a whole 4x4x4 slice. The times are simulated.
128 devices in a mesh: tm: 8 (over x, z_hi), rows: 16 (over z_lo, y, core).
Axes of the slice: x: 4, y: 4, z: 4 (z_hi: 2, z_lo: 2; z = z_hi * 2 + z_lo), core: 2. Of those that a mesh axis runs over, the one named last changes fastest.
Arguments:
- heights: bfloat16 [256, 1024, 1024], P('tm', 'rows'), may hold values from -6 to 6
Outputs:
- spectrum: float32 [64, 1024, 1024], P(None, ('tm', 'rows'))
All inputs are finite; a program needn't handle non-finite values.
Results may differ from a plain program's by a relative error of at most 0.0035.
Values may be sent and summed in bfloat16 or wider, within the bound.
A program may use at most 128 MiB of HBM per device.

v0:
```python
import functools
import math

import jax
import jax.numpy as jnp
from jax import lax
from jax.sharding import PartitionSpec as P


def spatial_table(length, tm_count, rows_count):
    column = jnp.arange(2 * length, dtype=jnp.int32)
    column_part = column % 2
    column_slot = column // 2
    per_device = length // (tm_count * rows_count)
    stride = tm_count * per_device
    owner_rank = column_slot // stride
    remainder = column_slot % stride
    wavenumber = (
        remainder // per_device * (length // tm_count)
        + owner_rank * per_device
        + remainder % per_device
    )
    position = jnp.arange(length, dtype=jnp.int32)
    angles = (position[:, None] * wavenumber[None, :] % length).astype(jnp.float32) * (
        2.0 * math.pi / length
    )
    values = jnp.where(column_part[None, :] == 0, jnp.cos(angles), -jnp.sin(angles))
    return (values / math.sqrt(length)).astype(jnp.bfloat16)


def make_column_table(length):
    position = jnp.arange(length, dtype=jnp.int32)
    angles = (position[:, None] * position[None, :] % length).astype(jnp.float32) * (
        2.0 * math.pi / length
    )
    values = jnp.concatenate([jnp.cos(angles), jnp.sin(angles)], 1)
    return (values / math.sqrt(length)).astype(jnp.bfloat16)


def time_table(window_len):
    time_step = jnp.arange(window_len, dtype=jnp.int32)
    hann_taper = 0.5 - 0.5 * jnp.cos(time_step.astype(jnp.float32) * (2.0 * math.pi / window_len))
    angles = (time_step[:, None] * time_step[None, :] % window_len).astype(jnp.float32) * (
        2.0 * math.pi / window_len
    )
    tables = jnp.stack(
        [jnp.cos(angles) * hann_taper[None, :], jnp.sin(angles) * hann_taper[None, :]], 0
    )
    return (tables.astype(jnp.bfloat16), jnp.sum(hann_taper * hann_taper))


def column_modes(mixed_rows, col_table):
    number, length, width = mixed_rows.shape
    block_size = math.gcd(number, max(1, 512 // width))

    def column_one_block(frame_block):
        product = jnp.einsum(
            "fxc,xk->fck", frame_block, col_table, preferred_element_type=jnp.float32
        )
        product = product.reshape(block_size, width // 2, 2, 2, length)
        real_part = product[:, :, 0, 0] + product[:, :, 1, 1]
        imag_part = product[:, :, 1, 0] - product[:, :, 0, 1]
        return jnp.stack([real_part, imag_part], 1).astype(jnp.bfloat16)

    result = lax.map(
        column_one_block, mixed_rows.reshape(number // block_size, block_size, length, width)
    )
    return result.reshape(number, 2, width // 2, length)


def window_pair(first_half, second_half, time_taper):
    hop_size = first_half.shape[0]
    number = first_half.shape[2]
    length = first_half.shape[3]
    block_size = math.gcd(number, 8)
    early_taper = time_taper[:, :, :hop_size]
    late_taper = time_taper[:, :, hop_size:]

    def window_one_block(block_index, accumulated):
        product = jnp.einsum(
            "swt,tpqx->swpqx", early_taper, first_half, preferred_element_type=jnp.float32
        )
        product = product + jnp.einsum(
            "swt,tpqx->swpqx", late_taper, second_half, preferred_element_type=jnp.float32
        )
        real_part = product[0, :, 0] + product[1, :, 1]
        imag_part = product[0, :, 1] - product[1, :, 0]
        return real_part * real_part + imag_part * imag_part

    start = jnp.zeros((time_taper.shape[1], number, length), jnp.float32)
    return lax.fori_loop(0, number // block_size, window_one_block, start)


def all_windows(mode_field, time_taper, hop_size):
    block_count = mode_field.shape[0] // hop_size
    blocks = mode_field.reshape((block_count, hop_size) + mode_field.shape[1:])

    def one_window(window_index, accumulated):
        first_half = lax.dynamic_index_in_dim(blocks, window_index, 0, keepdims=False)
        second_half = lax.dynamic_index_in_dim(blocks, window_index + 1, 0, keepdims=False)
        return accumulated + window_pair(first_half, second_half, time_taper)

    start = jnp.zeros((time_taper.shape[1], mode_field.shape[2], mode_field.shape[3]), jnp.float32)
    return lax.fori_loop(0, block_count - 1, one_window, start)


def body(heights):
    frames, rows_dev, length = heights.shape
    tm_count = lax.axis_size("tm")
    rows_count = lax.axis_size("rows")
    time_taper, energy = time_table(2 * frames)
    row_table, col_table = lax.optimization_barrier(
        (spatial_table(length, tm_count, rows_count), make_column_table(length))
    )
    mixed_rows = jnp.dot(
        heights.reshape(frames * rows_dev, length), row_table, preferred_element_type=jnp.float32
    )
    mixed_rows = mixed_rows.astype(jnp.bfloat16).reshape(frames, rows_dev, 2 * length)
    transform = functools.partial(column_modes, col_table=col_table)
    mode_field = transform(
        lax.all_to_all(mixed_rows, "rows", split_axis=2, concat_axis=1, tiled=True)
    )
    windows_fn = functools.partial(all_windows, time_taper=time_taper, hop_size=frames)
    summed = windows_fn(lax.all_to_all(mode_field, "tm", split_axis=2, concat_axis=0, tiled=True))
    return summed / ((tm_count - 1) * energy)


def solution(mesh):
    in_specs = (P("tm", "rows", None),)
    out_specs = P(None, ("tm", "rows"), None)
    return jax.shard_map(body, mesh=mesh, in_specs=in_specs, out_specs=out_specs, check_vma=False)
```

profile of v0, /device:TPU:8, one launch (start us, length us, event | category | flops | bytes accessed | tf_op | source)
XLA Modules:
  0.0 607.7 jit_solution(6191324189082903849)
XLA Ops:
  0.0 16.3 %fusion.36 = (f32[1024,1024]{0,1:T(8,128)S(1)}, f32[1024,1024]{0,1:T(8,128)S(1)}) fusion(), kind=kLoop, calls=%fused_computation.55 | loop fusion | flops 14680064 | bytes 8388608 | tf_op jit(solution)/shard_map/sin | solution.py:36
  16.4 2.7 fusion.26
  19.1 36.0 %multiply_convert_fusion = bf16[1024,2048]{0,1:T(8,128)(2,1)S(1)} fusion(s32[2048]{0:T(1024)S(1)} %fusion.51, pred[2048]{0:T(1024)(128)(4,1)S(1)} %fusion.44), kind=kLoop, calls=%fused_computation.41 | loop fusion | flops 37748736 | bytes 4204544 | tf_op jit(solution)/shard_map/convert_element_type | solution.py:28
  55.2 11.4 %convolution_convert_fusion = bf16[2048,2048]{0,1:T(8,128)(2,1)} fusion(bf16[1024,2048]{0,1:T(8,128)(2,1)S(1)} %multiply_convert_fusion, bf16[2048,1024]{1,0:T(8,128)(2,1)S(1)} %bitcast.114), kind=kOutput, calls=%fused_computation.45 | convolution fusion | flops 8594128896 | bytes 16777216 | tf_op jit(solution)/shard_map/dot_general | solution.py:115
  66.6 23.9 %copy.34 = bf16[32,64,2048]{1,0,2:T(8,128)(2,1)} copy(bf16[32,64,2048]{2,1,0:T(8,128)(2,1)} %bitcast.111) | data formatting | bytes 16777216 | tf_op jit(solution)/shard_map/reshape | solution.py:118
  90.5 19.6 %reshape.318 = bf16[16,2,131072]{2,1,0:T(2,128)(2,1)} reshape(bf16[2048,32,64]{2,1,0:T(8,128)(2,1)} %bitcast.106) | data formatting | bytes 16777216
  110.1 6.3 %all-to-all-start = ((bf16[16,2,131072]{2,1,0:T(2,128)(2,1)}), bf16[16,2,131072]{2,1,0:T(2,128)(2,1)}, u32[]{:S(2)}, u32[]{:S(2)}) async-start(bf16[16,2,131072]{2,1,0:T(2,128)(2,1)} %reshape.318), calls=%async_computation | async-start | bytes 16777216 | tf_op jit(solution)/shard_map/all_to_all | solution.py:121
  116.4 113.5 %all-to-all-done = bf16[16,2,131072]{2,1,0:T(2,128)(2,1)} async-done(((bf16[16,2,131072]{2,1,0:T(2,128)(2,1)}), bf16[16,2,131072]{2,1,0:T(2,128)(2,1)}, u32[]{:S(2)}, u32[]{:S(2)}) %all-to-all-start) | async-done | bytes 8388640 | tf_op jit(solution)/shard_map/all_to_all | solution.py:121
  229.9 19.3 %reshape.319 = bf16[2048,32,64]{2,1,0:T(8,128)(2,1)} reshape(bf16[16,2,131072]{2,1,0:T(2,128)(2,1)} %all-to-all-done) | data formatting | bytes 16777216
  249.2 18.4 %copy.36 = bf16[32,16,64,128]{3,2,1,0:T(8,128)(2,1)} copy(bf16[32,16,64,128]{2,0,3,1:T(8,128)(2,1)} %bitcast.107) | data formatting | bytes 16777216 | tf_op jit(solution)/shard_map/all_to_all | solution.py:121
  267.6 71.1 %while.34 = (s32[]{:T(128)}, bf16[8,4,2,64,1024]{4,3,2,1,0:T(8,128)(2,1)}, bf16[8,4,1024,128]{3,2,1,0:T(8,128)(2,1)}, bf16[1024,2048]{0,1:T(8,128)(2,1)}, s32[]{:T(128)}) while((s32[]{:T(128)}, bf16[8,4,2,64,1024]{4,3,2,1,0:T(8,128)(2,1)}, bf16[8,4,1024,128]{3,2,1,0:T(8,128)(2,1)}, bf16[1024,2048]{0,1:T(8,128)(2,1)}, s32[]{:T(128)}) %tuple.74), condition=%wide.region_1.2_spmd, body=%wide.region_0.1_spmd.sunk | while | flops 2149056512 | bytes 20972096 | solution.py:65
  267.6 1.3 constant_dynamic-slice_fusion.2
  269.8 5.3 fusion.79
  275.4 1.1 copy_dynamic-update-slice_fusion.2
  276.5 1.3 constant_dynamic-slice_fusion.2
  278.7 5.3 fusion.79
  284.3 1.1 copy_dynamic-update-slice_fusion.2
  285.4 1.3 constant_dynamic-slice_fusion.2
  286.7 0.9 copy.69
  287.6 5.3 fusion.79
  293.2 1.1 copy_dynamic-update-slice_fusion.2
  294.3 1.3 constant_dynamic-slice_fusion.2
  296.5 5.3 fusion.79
  302.1 1.1 copy_dynamic-update-slice_fusion.2
  303.2 1.3 constant_dynamic-slice_fusion.2
  305.4 5.3 fusion.79
  311.0 1.2 copy_dynamic-update-slice_fusion.2
  312.1 1.3 constant_dynamic-slice_fusion.2
  314.4 5.3 fusion.79
  319.9 1.1 copy_dynamic-update-slice_fusion.2
  321.0 1.3 constant_dynamic-slice_fusion.2
  323.2 5.3 fusion.79
  328.8 1.1 copy_dynamic-update-slice_fusion.2
  329.9 1.3 constant_dynamic-slice_fusion.2
  332.1 5.3 fusion.79
  337.6 1.1 copy_dynamic-update-slice_fusion.2
  338.8 16.4 %copy.39 = bf16[32,2,64,1024]{3,1,0,2:T(2,128)(2,1)} copy(bf16[32,2,64,1024]{3,2,1,0:T(8,128)(2,1)} %bitcast.112) | data formatting | bytes 16777216 | tf_op jit(solution)/shard_map/reshape | solution.py:68
  355.1 7.3 %all-to-all-start.1 = ((bf16[32,2,64,1024]{3,1,0,2:T(2,128)(2,1)}), bf16[32,2,64,1024]{3,1,0,2:T(2,128)(2,1)}, u32[]{:S(2)}, u32[]{:S(2)}) async-start(bf16[32,2,64,1024]{3,1,0,2:T(2,128)(2,1)} %copy.39), calls=%async_computation.1 | async-start | bytes 16777216 | tf_op jit(solution)/shard_map/all_to_all | solution.py:124
  364.2 114.2 %all-to-all-done.1 = bf16[32,2,64,1024]{3,1,0,2:T(2,128)(2,1)} async-done(((bf16[32,2,64,1024]{3,1,0,2:T(2,128)(2,1)}), bf16[32,2,64,1024]{3,1,0,2:T(2,128)(2,1)}, u32[]{:S(2)}, u32[]{:S(2)}) %all-to-all-start.1) | async-done | bytes 8388640 | tf_op jit(solution)/shard_map/all_to_all | solution.py:124
  478.3 13.5 %copy.63 = bf16[32,2,64,1024]{3,2,1,0:T(8,128)(2,1)} copy(bf16[32,2,64,1024]{3,1,0,2:T(2,128)(2,1)} %all-to-all-done.1) | data formatting | bytes 16777216 | tf_op jit(solution)/shard_map/all_to_all | solution.py:124
  491.8 12.4 %copy.41 = bf16[8,32,2,8,1024]{4,1,3,2,0:T(8,128)(2,1)} copy(bf16[8,32,2,8,1024]{4,3,0,2,1:T(8,128)(2,1)} %bitcast.108) | data formatting | bytes 16777216
  504.2 100.5 %while.35 = (s32[]{:T(128)}, f32[64,8,1024]{2,0,1:T(8,128)S(1)}, bf16[8,32,2,8,1024]{4,1,3,2,0:T(8,128)(2,1)}, bf16[2,64,64]{1,2,0:T(8,128)(2,1)S(1)}, s32[]{:T(128)}, /*index=5*/s32[]{:T(128)}, s32[]{:T(128)}) while((s32[]{:T(128)}, f32[64,8,1024]{2,0,1:T(8,128)S(1)}, bf16[8,32,2,8,1024]{4,1,3,2,0:T(8,128)(2,1)}, ...), condition=%wide.region_3.4_spmd.clone, body=%wide.region_2.3_spmd.clone.sunk | while | flops 274202624 | bytes 39879300 | solution.py:104
  504.2 2.6 fusion.86
  506.8 6.7 %add_bitcast_fusion.2 = f32[2,64,2,8,1024]{4,1,0,3,2:T(8,128)} fusion(f32[2,8,1024,2,64]{2,4,3,1,0:T(8,128)S(1)} %fusion.86, bf16[8,32,2,8,1024]{4,1,3,2,0:T(8,128)(2,1)} %get-tuple-element.314, s32[]{:T(128)S(6)} %select_n.183, bf16[2,64,64]{1,2,0:T(8,128)(2,1)S(1)} %get-tuple-element.315), kind=kOutput, calls=%fused_computation.13.clone.1 | convolution fusion | flops 136314880 | bytes 17842180 | tf_op jit(solution)/shard_map/while/body/eval_jaxpr/while/body/eval_jaxpr/swt,tpqx->swpqx/dot_general | solution.py:83
  513.5 5.0 fusion.87
  518.6 2.6 fusion.86
  521.2 6.7 %add_bitcast_fusion.2 = f32[2,64,2,8,1024]{4,1,0,3,2:T(8,128)} fusion(f32[2,8,1024,2,64]{2,4,3,1,0:T(8,128)S(1)} %fusion.86, bf16[8,32,2,8,1024]{4,1,3,2,0:T(8,128)(2,1)} %get-tuple-element.314, s32[]{:T(128)S(6)} %select_n.183, bf16[2,64,64]{1,2,0:T(8,128)(2,1)S(1)} %get-tuple-element.315), kind=kOutput, calls=%fused_computation.13.clone.1 | convolution fusion | flops 136314880 | bytes 17842180 | tf_op jit(solution)/shard_map/while/body/eval_jaxpr/while/body/eval_jaxpr/swt,tpqx->swpqx/dot_general | solution.py:83
  527.9 5.0 fusion.87
  532.9 2.6 fusion.86
  535.5 6.7 %add_bitcast_fusion.2 = f32[2,64,2,8,1024]{4,1,0,3,2:T(8,128)} fusion(f32[2,8,1024,2,64]{2,4,3,1,0:T(8,128)S(1)} %fusion.86, bf16[8,32,2,8,1024]{4,1,3,2,0:T(8,128)(2,1)} %get-tuple-element.314, s32[]{:T(128)S(6)} %select_n.183, bf16[2,64,64]{1,2,0:T(8,128)(2,1)S(1)} %get-tuple-element.315), kind=kOutput, calls=%fused_computation.13.clone.1 | convolution fusion | flops 136314880 | bytes 17842180 | tf_op jit(solution)/shard_map/while/body/eval_jaxpr/while/body/eval_jaxpr/swt,tpqx->swpqx/dot_general | solution.py:83
  542.2 5.0 fusion.87
  547.3 2.6 fusion.86
  549.9 6.7 %add_bitcast_fusion.2 = f32[2,64,2,8,1024]{4,1,0,3,2:T(8,128)} fusion(f32[2,8,1024,2,64]{2,4,3,1,0:T(8,128)S(1)} %fusion.86, bf16[8,32,2,8,1024]{4,1,3,2,0:T(8,128)(2,1)} %get-tuple-element.314, s32[]{:T(128)S(6)} %select_n.183, bf16[2,64,64]{1,2,0:T(8,128)(2,1)S(1)} %get-tuple-element.315), kind=kOutput, calls=%fused_computation.13.clone.1 | convolution fusion | flops 136314880 | bytes 17842180 | tf_op jit(solution)/shard_map/while/body/eval_jaxpr/while/body/eval_jaxpr/swt,tpqx->swpqx/dot_general | solution.py:83
  556.6 5.0 fusion.87
  561.6 2.6 fusion.86
  564.2 6.7 %add_bitcast_fusion.2 = f32[2,64,2,8,1024]{4,1,0,3,2:T(8,128)} fusion(f32[2,8,1024,2,64]{2,4,3,1,0:T(8,128)S(1)} %fusion.86, bf16[8,32,2,8,1024]{4,1,3,2,0:T(8,128)(2,1)} %get-tuple-element.314, s32[]{:T(128)S(6)} %select_n.183, bf16[2,64,64]{1,2,0:T(8,128)(2,1)S(1)} %get-tuple-element.315), kind=kOutput, calls=%fused_computation.13.clone.1 | convolution fusion | flops 136314880 | bytes 17842180 | tf_op jit(solution)/shard_map/while/body/eval_jaxpr/while/body/eval_jaxpr/swt,tpqx->swpqx/dot_general | solution.py:83
  570.9 5.0 fusion.87
  576.0 2.6 fusion.86
  578.6 6.7 %add_bitcast_fusion.2 = f32[2,64,2,8,1024]{4,1,0,3,2:T(8,128)} fusion(f32[2,8,1024,2,64]{2,4,3,1,0:T(8,128)S(1)} %fusion.86, bf16[8,32,2,8,1024]{4,1,3,2,0:T(8,128)(2,1)} %get-tuple-element.314, s32[]{:T(128)S(6)} %select_n.183, bf16[2,64,64]{1,2,0:T(8,128)(2,1)S(1)} %get-tuple-element.315), kind=kOutput, calls=%fused_computation.13.clone.1 | convolution fusion | flops 136314880 | bytes 17842180 | tf_op jit(solution)/shard_map/while/body/eval_jaxpr/while/body/eval_jaxpr/swt,tpqx->swpqx/dot_general | solution.py:83
  585.3 5.0 fusion.87
  590.4 2.6 fusion.86
  592.9 6.7 %add_bitcast_fusion.2 = f32[2,64,2,8,1024]{4,1,0,3,2:T(8,128)} fusion(f32[2,8,1024,2,64]{2,4,3,1,0:T(8,128)S(1)} %fusion.86, bf16[8,32,2,8,1024]{4,1,3,2,0:T(8,128)(2,1)} %get-tuple-element.314, s32[]{:T(128)S(6)} %select_n.183, bf16[2,64,64]{1,2,0:T(8,128)(2,1)S(1)} %get-tuple-element.315), kind=kOutput, calls=%fused_computation.13.clone.1 | convolution fusion | flops 136314880 | bytes 17842180 | tf_op jit(solution)/shard_map/while/body/eval_jaxpr/while/body/eval_jaxpr/swt,tpqx->swpqx/dot_general | solution.py:83
  599.7 5.0 fusion.87
  604.9 2.5 copy.43
  (34 shorter events, 9.9 us)
Async XLA Ops:
  19.1 36.1 %copy-start = (bf16[32,64,1024]{2,1,0:T(8,128)(2,1)S(1)}, bf16[32,64,1024]{2,1,0:T(8,128)(2,1)}, u32[]{:S(2)}) copy-start(bf16[32,64,1024]{2,1,0:T(8,128)(2,1)} %param.5) | copy-start | bytes 12582916
  110.1 119.8 %all-to-all-start = ((bf16[16,2,131072]{2,1,0:T(2,128)(2,1)}), bf16[16,2,131072]{2,1,0:T(2,128)(2,1)}, u32[]{:S(2)}, u32[]{:S(2)}) async-start(bf16[16,2,131072]{2,1,0:T(2,128)(2,1)} %reshape.318), calls=%async_computation | async-start | bytes 16777216 | tf_op jit(solution)/shard_map/all_to_all | solution.py:121
  355.1 123.2 %all-to-all-start.1 = ((bf16[32,2,64,1024]{3,1,0,2:T(2,128)(2,1)}), bf16[32,2,64,1024]{3,1,0,2:T(2,128)(2,1)}, u32[]{:S(2)}, u32[]{:S(2)}) async-start(bf16[32,2,64,1024]{3,1,0,2:T(2,128)(2,1)} %copy.39), calls=%async_computation.1 | async-start | bytes 16777216 | tf_op jit(solution)/shard_map/all_to_all | solution.py:124
where the time goes:
time: 619 us; the launch traced here: 608 us
  waiting for transfers between devices  228 us (37%)
  local copies, waits for them, and re-layouts  144 us (23%)
  matrix products  119 us (19%)
  other arithmetic  103 us (17%)
  starting transfers between devices  13.6 us (2%)
    all_to_all x1, waiting for transfers between devices, body(): lax.all_to_all(mode_field, 'tm', split_axis=2, concat_axis=0, tiled=True)  114 us
    all_to_all x1, waiting for transfers between devices, body(): lax.all_to_all(mixed_rows, 'rows', split_axis=2, concat_axis=1, tiled=True)  113 us
    unnamed x5, local copies, waits for them, and re-layouts  51.3 us
    dot_general x7, matrix products, window_one_block(): jnp.einsum('swt,tpqx->swpqx', late_taper, second_half, preferred_element_...  47 us
    dot_general x8, matrix products, column_one_block(): jnp.einsum('fxc,xk->fck', frame_block, col_table, preferred_element_type=...  42.1 us
    convert_element_type x1, other arithmetic, spatial_table(): return (values / math.sqrt(length)).astype(jnp.bfloat16)  36 us
    add x7, other arithmetic, one_window(): return accumulated + window_pair(first_half, second_half, time_taper)  35.2 us
    reshape x1, local copies, waits for them, and re-layouts, body(): mixed_rows.astype(jnp.bfloat16).reshape(frames, rows_dev, 2 * length)  23.9 us
  transfers between devices with their start and end apart: 2, of which 2 were waited for; matrix products, arithmetic and copies ran while one was open for 0% of the time, Pallas kernels for 0%

commit v1 on v0

v1 whole, which is shorter than its diff:
```python
import functools
import math

import jax
import jax.numpy as jnp
import ml_dtypes
import numpy as np
from jax import lax
from jax.experimental import pallas as pl
from jax.experimental.pallas import tpu as pltpu
from jax.sharding import PartitionSpec as P

MESH = pl.DeviceIdType.MESH
GRID = 1024
HALF = 512
WIN = 64
TM = 8
ROWS = 16
DEVICES = TM * ROWS
FRAMES_DEV = 32
X_DEV = 64
BF16 = jnp.bfloat16
F32 = jnp.float32


def trig(index):
    angles = (index % GRID).astype(np.float32) * np.float32(2.0 * math.pi / GRID)
    scale = np.float32(math.sqrt(GRID))
    return np.cos(angles) / scale, np.sin(angles) / scale


def row_table():
    row = np.arange(HALF)
    pair, part, parity, low = row // 8, row // 4 % 2, row // 2 % 2, row % 2
    device = 2 * pair + parity
    y = np.arange(HALF)
    tables = []
    for phase in range(2):
        slot = 2 * phase + low
        q = np.where(device < 64, 8 * device + slot, 8 * (127 - device) + 4 + slot)
        cosine, sine = trig(q[:, None] * y[None, :])
        values = np.where(part[:, None] == 0, cosine, -sine)
        shared = (device == 0) & (slot == 0) & (part == 1)
        nyquist, _ = trig(HALF * y)
        tables.append(np.where(shared[:, None], nyquist[None, :], values))
    return np.stack(tables).astype(ml_dtypes.bfloat16)


def column_table():
    x = np.arange(HALF)
    cosine, sine = trig(x[:, None] * x[None, :])
    sine[:, 0] = trig(x * HALF)[0]
    return np.concatenate([cosine, sine], 1).astype(ml_dtypes.bfloat16)


def tapers():
    t = np.arange(WIN)
    hann = np.float32(0.5) - np.float32(0.5) * np.cos(
        t.astype(np.float32) * np.float32(2.0 * math.pi / WIN)
    )
    angles = (t[:, None] * t[None, :] % WIN).astype(np.float32) * np.float32(2.0 * math.pi / WIN)
    energy = float(np.sum(hann * hann, dtype=np.float32))

    def rounded(values):
        return (values * hann[None, :]).astype(ml_dtypes.bfloat16).astype(np.float32)

    return rounded(np.cos(angles)), rounded(np.sin(angles)), energy


def time_matrices():
    cosine, sine, _ = tapers()
    k = np.arange(256)
    block, second, inner = k // 128, k // 64 % 2, k // 16 % 4
    high, part, low, slot = k // 8 % 2, k // 4 % 2, k // 2 % 2, k % 2
    t = 32 * block + 8 * (2 * high + low) + 2 * inner + second
    real = np.where(part == 0, cosine[:, t], sine[:, t])
    imag = np.where(part == 0, -sine[:, t], cosine[:, t])
    rows = [np.where(slot == s, m, 0.0) for s in range(2) for m in (real, imag)]
    back = (-np.arange(WIN)) % WIN
    first = rows[:2] + [rows[0][back], rows[1][back]]
    return (
        np.concatenate(rows).astype(ml_dtypes.bfloat16),
        np.concatenate(first).astype(ml_dtypes.bfloat16),
    )


def peer_of(step, tm, rows):
    x, z = tm // 2, (tm % 2) * 2 + rows // 8
    y, core = rows // 2 % 4, rows % 2
    shift = step * 91 % DEVICES
    x = (x + shift // 32) % 4
    y = (y + shift // 8 % 4) % 4
    z = (z + shift // 2 % 4) % 4
    core = (core + shift % 2) % 2
    return x * 2 + z // 2, (z % 2 * 4 + y) * 2 + core


def spectrum_kernel(
    h_ref, ty_ref, tx_ref, time_ref, time0_ref, own_ref, got_ref,
    tab, txa, txb, rowsum, send, recv, lhs, rc, rs, modes, msg,
    send_sem, recv_sem, local_sem, msg_send_sem, msg_recv_sem,
):
    tm, rows = lax.axis_index("tm"), lax.axis_index("rows")
    me = tm * ROWS + rows
    core = rows % 2

    def device(target):
        return {"tm": target // ROWS, "rows": target % ROWS}

    barrier = pltpu.get_barrier_semaphore()

    @pl.loop(1, DEVICES)
    def _(step):
        pl.semaphore_signal(
            barrier, inc=1, device_id=device((me + step) % DEVICES), device_id_type=MESH
        )

    row_sign = jnp.where(lax.broadcasted_iota(jnp.int32, (HALF, 1), 0) % 2 == 0, 1.0, -1.0)
    for phase in range(2):
        tab[phase, :, :HALF] = ty_ref[phase]
        tab[phase, :, HALF:] = (ty_ref[phase].astype(F32) * row_sign).astype(BF16)
    lane_sign = jnp.where(lax.broadcasted_iota(jnp.int32, (1, GRID), 1) % 2 == 0, 1.0, -1.0)
    txa[:HALF] = tx_ref[...]
    txa[HALF:] = (tx_ref[...].astype(F32) * lane_sign).astype(BF16)

    @pl.loop(0, 8)
    def _(block):
        base = pl.multiple_of(block * 128, 128)
        txb[pl.ds(base, 64)] = txa[pl.ds(base + 64, 64)]
        txb[pl.ds(base + 64, 64)] = txa[pl.ds(base, 64)]

    def row_phase(phase):
        for inner in range(2):
            lanes = slice(inner * 256, inner * 256 + 256)

            @pl.loop(0, 4)
            def _(quarter):
                base = quarter * 8 + inner * 4
                block = jnp.concatenate(
                    [
                        h_ref[base + core],
                        h_ref[base + 1 - core],
                        h_ref[base + 2 + core],
                        h_ref[base + 3 - core],
                    ],
                    0,
                )
                rowsum[quarter] = lax.dot_general(
                    tab[phase], block, (((1,), (1,)), ((), ())), preferred_element_type=F32
                )

            @pl.loop(0, 8)
            def _(part):
                at = pl.ds(pl.multiple_of(part * 64, 64), 64)
                pieces = [rowsum[f, at].reshape(8, 8, 256) for f in range(4)]
                early = lax.broadcasted_iota(jnp.int32, (8, 8, 256), 1) // 2 % 2 == 0
                evens, odds = [], []
                for a, b in ((pieces[0], pieces[1]), (pieces[2], pieces[3])):
                    evens.append(jnp.where(early, a, pltpu.roll(b, 2, 1)))
                    odds.append(jnp.where(early, pltpu.roll(a, 6, 1), b))
                pairs = pl.ds(part * 8, 8)
                send[phase, pairs, 0, :, lanes] = jnp.concatenate(evens, 1).astype(BF16)
                send[phase, pairs, 1, :, lanes] = jnp.concatenate(odds, 1).astype(BF16)

    def start_sends(phase):
        @pl.loop(1, DEVICES)
        def _(step):
            to_tm, to_rows = peer_of(step, tm, rows)
            target = to_tm * ROWS + to_rows
            pltpu.make_async_remote_copy(
                src_ref=send.at[phase, target // 2, target % 2],
                dst_ref=recv.at[phase, me],
                send_sem=send_sem.at[phase],
                recv_sem=recv_sem.at[phase],
                device_id={"tm": to_tm, "rows": to_rows},
                device_id_type=MESH,
            ).start()

        pltpu.make_async_copy(
            send.at[phase, me // 2, me % 2], recv.at[phase, me], local_sem.at[phase]
        ).start()

    def wait_all(phase, sem):
        blocks = recv.at[phase, pl.ds(0, DEVICES - 1)]
        pltpu.make_async_copy(blocks, blocks, sem.at[phase]).wait()

    def column_phase(phase):
        @pl.loop(0, TM)
        def _(block):
            low = lax.broadcasted_iota(jnp.int32, (16, 512), 1) % 128 < 64
            for pair in range(8):
                even = recv[phase, block * ROWS + 2 * pair]
                odd = recv[phase, block * ROWS + 2 * pair + 1]
                first = jnp.where(low, even, odd)
                second = jnp.where(low, odd, even)
                for inner in range(4):
                    at = pl.ds(pl.multiple_of(block * 64 + inner * 16, 16), 16)
                    lanes = slice(inner * 128, inner * 128 + 128)
                    columns = slice(pair * 128, pair * 128 + 128)
                    lhs[0, at, columns] = first[:, lanes]
                    lhs[1, at, columns] = second[:, lanes]

        for second in range(2):
            table = txb if second else txa
            for part in range(2):
                columns = slice(part * 256, part * 256 + 256)
                above = slice(HALF + part * 256, HALF + part * 256 + 256)
                rc[...] = jnp.dot(lhs[second], table[:, columns], preferred_element_type=F32)
                rs[...] = jnp.dot(lhs[second], table[:, above], preferred_element_type=F32)

                @pl.loop(0, TM)
                def _(block):
                    at = pl.ds(pl.multiple_of(block * 64, 64), 64)
                    cosine = rc[at].reshape(8, 8, 256)
                    sine = rs[at].reshape(8, 8, 256)
                    top = lax.broadcasted_iota(jnp.int32, (8, 8, 256), 1) < 4
                    swapped = pltpu.roll(sine, 4, 1)
                    swapped = jnp.where(top, swapped, -swapped)
                    plus, minus = cosine + swapped, cosine - swapped
                    if part == 0:
                        edge = lax.broadcasted_iota(jnp.int32, (8, 8, 256), 2) == 0
                        plus = jnp.where(edge, cosine, plus)
                        minus = jnp.where(edge, sine, minus)
                    modes[block, second, :, columns] = plus.reshape(64, 256).astype(BF16)
                    modes[block, second, :, above] = minus.reshape(64, 256).astype(BF16)

    def time_phase(phase):
        @pl.loop(0, 4)
        def _(part):
            columns = pl.ds(pl.multiple_of(part * 256, 256), 256)
            total = None
            for window in range(TM - 1):
                u = jnp.dot(
                    time_ref[...],
                    modes[pl.ds(window, 2), :, :, columns].reshape(256, 256),
                    preferred_element_type=F32,
                )
                u = u * u
                power = jnp.concatenate([u[:64] + u[64:128], u[128:192] + u[192:]], 0)
                total = power if total is None else total + power
            for low in range(2):
                piece = total[low * 64 : low * 64 + 64]
                own_ref[2 * phase + low, :, columns] = piece
                msg[2 * phase + low, :, columns] = piece.astype(BF16)

        if phase == 0:
            @pl.when(me == 0)
            def _():
                @pl.loop(0, 2)
                def _(part):
                    columns = pl.ds(pl.multiple_of(part * 256, 256), 256)
                    above = pl.ds(pl.multiple_of(HALF + part * 256, 256), 256)
                    lane = lax.broadcasted_iota(jnp.int32, (128, 256), 1) + part * 256
                    sums = [None] * 4
                    for window in range(TM - 1):
                        a, b = (
                            jnp.dot(
                                time0_ref[...],
                                modes[pl.ds(window, 2), :, :, at].reshape(256, 256),
                                preferred_element_type=F32,
                            )
                            for at in (columns, above)
                        )
                        back_a = jnp.where(lane == 0, a[128:], b[128:])
                        back_b = jnp.where(lane == 0, b[128:], a[128:])
                        terms = []
                        for here, back in ((a[:128], back_a), (b[:128], back_b)):
                            r, i, rb, ib = here[:64], here[64:], back[:64], back[64:]
                            terms.append((r + rb) * (r + rb) + (i - ib) * (i - ib))
                            terms.append((r - rb) * (r - rb) + (i + ib) * (i + ib))
                        sums = [t if s is None else s + t for s, t in zip(sums, terms)]
                    own_ref[0, :, columns] = sums[0] * 0.25
                    own_ref[0, :, above] = sums[2] * 0.25
                    msg[0, :, columns] = (sums[1] * 0.25).astype(BF16)
                    msg[0, :, above] = (sums[3] * 0.25).astype(BF16)

    mirror = DEVICES - 1 - me
    first_to = jnp.where(me == 0, 64, jnp.where(me < 64, DEVICES - me, mirror))

    def message(slot):
        return pltpu.make_async_remote_copy(
            src_ref=msg.at[slot],
            dst_ref=got_ref.at[slot],
            send_sem=msg_send_sem.at[slot],
            recv_sem=msg_recv_sem.at[slot],
            device_id=device(first_to if slot == 0 else mirror),
            device_id_type=MESH,
        )

    row_phase(0)
    pl.semaphore_wait(barrier, DEVICES - 1)
    start_sends(0)
    row_phase(1)
    start_sends(1)
    for phase in range(2):
        pltpu.make_async_copy(
            send.at[phase, me // 2, me % 2], recv.at[phase, me], local_sem.at[phase]
        ).wait()
        wait_all(phase, recv_sem)
        column_phase(phase)
        time_phase(phase)
        for low in range(2):
            message(2 * phase + low).start()
    for phase in range(2):
        wait_all(phase, send_sem)
    for slot in range(4):
        message(slot).wait()


def final_kernel(scale, own_ref, got_ref, out_ref, stack, left, flip):
    me = lax.axis_index("tm") * ROWS + lax.axis_index("rows")
    upper = me >= 64
    i = lax.broadcasted_iota(jnp.int32, (HALF, HALF), 0)
    j = lax.broadcasted_iota(jnp.int32, (HALF, HALF), 1)
    flip[...] = jnp.where(i == (HALF - j) % HALF, 1.0, 0.0).astype(BF16)
    to = lax.broadcasted_iota(jnp.int32, (HALF, 256), 0)
    come = lax.broadcasted_iota(jnp.int32, (HALF, 256), 1)
    w, row = to // 8, to % 8
    w_from = jnp.where(upper, (WIN - w) % WIN, w)
    slot_own = jnp.where(upper, jnp.where((row >= 1) & (row <= 4), 4 - row, -1), jnp.where(row < 4, row, -1))
    slot_got = jnp.where(
        upper, jnp.where(row == 0, 0, jnp.where(row >= 5, 8 - row, -1)), jnp.where(row >= 4, row - 4, -1)
    )
    own_map = jnp.where((come // WIN == slot_own) & (come % WIN == w_from), 1.0, 0.0).astype(BF16)
    left[:, :256] = own_map
    left[:, 256:512] = own_map
    left[:, 512:] = jnp.where((come // WIN == slot_got) & (come % WIN == w_from), 1.0, 0.0).astype(BF16)
    swap = (lax.broadcasted_iota(jnp.int32, (256, HALF), 1) >= 1) & upper

    def place(at, a, b):
        stack[at, :HALF] = jnp.where(swap, b, a).astype(BF16)
        other = jnp.where(swap, a, b).astype(BF16)
        stack[at, HALF:] = jnp.dot(other, flip[...], preferred_element_type=F32).astype(BF16)

    a, b = own_ref[:, :HALF], own_ref[:, HALF:]
    a_top, b_top = a.astype(BF16).astype(F32), b.astype(BF16).astype(F32)
    place(slice(0, 256), a_top, b_top)
    place(slice(256, 512), a - a_top, b - b_top)
    place(slice(512, 768), got_ref[:, :HALF].astype(F32), got_ref[:, HALF:].astype(F32))

    for part in range(4):
        columns = slice(part * 256, part * 256 + 256)
        result = jnp.dot(left[...], stack[:, columns], preferred_element_type=F32) * scale
        out_ref[:, :, columns] = result.reshape(WIN, 8, 256)


def body(heights):
    vmem = pl.BlockSpec(memory_space=pltpu.VMEM)
    time_matrix, time_first = time_matrices()
    energy = tapers()[2]
    dma = pltpu.SemaphoreType.DMA
    own, got = pl.pallas_call(
        spectrum_kernel,
        out_shape=(
            jax.ShapeDtypeStruct((4, WIN, GRID), F32),
            jax.ShapeDtypeStruct((4, WIN, GRID), BF16),
        ),
        in_specs=[vmem] * 5,
        out_specs=(vmem, vmem),
        scratch_shapes=[
            pltpu.VMEM((2, HALF, GRID), BF16),
            pltpu.VMEM((GRID, GRID), BF16),
            pltpu.VMEM((GRID, GRID), BF16),
            pltpu.VMEM((4, HALF, 256), F32),
            pltpu.VMEM((2, DEVICES // 2, 2, 16, 512), BF16),
            pltpu.VMEM((2, DEVICES, 16, 512), BF16),
            pltpu.VMEM((2, HALF, GRID), BF16),
            pltpu.VMEM((HALF, 256), F32),
            pltpu.VMEM((HALF, 256), F32),
            pltpu.VMEM((TM, 2, 64, GRID), BF16),
            pltpu.VMEM((4, WIN, GRID), BF16),
            dma((2,)),
            dma((2,)),
            dma((2,)),
            dma((4,)),
            dma((4,)),
        ],
        compiler_params=pltpu.CompilerParams(
            collective_id=0, has_side_effects=True, vmem_limit_bytes=60 << 20
        ),
    )(
        heights,
        jnp.asarray(row_table()),
        jnp.asarray(column_table()),
        jnp.asarray(time_matrix),
        jnp.asarray(time_first),
    )
    return pl.pallas_call(
        functools.partial(final_kernel, 1.0 / ((TM - 1) * energy)),
        out_shape=jax.ShapeDtypeStruct((WIN, 8, GRID), F32),
        in_specs=[vmem, vmem],
        out_specs=vmem,
        scratch_shapes=[
            pltpu.VMEM((768, GRID), BF16),
            pltpu.VMEM((HALF, 768), BF16),
            pltpu.VMEM((HALF, HALF), BF16),
        ],
        compiler_params=pltpu.CompilerParams(vmem_limit_bytes=40 << 20),
    )(own.reshape(256, GRID), got.reshape(256, GRID))


def solution(mesh):
    return jax.shard_map(
        body,
        mesh=mesh,
        in_specs=(P("tm", "rows", None),),
        out_specs=P(None, ("tm", "rows"), None),
        check_vma=False,
    )
```

time: 619 us -> 87.4 us (0.14)
  the two profiles are of different devices: /device:TPU:8 before, /device:TPU:105 now
where the time goes in v1:
time: 87.4 us; the launch traced here: 87.2 us
  Pallas kernels  84.9 us (97%)
  local copies, waits for them, and re-layouts  2.26 us (3%)
    pallas_call x1, Pallas kernels, body(): pl.pallas_call(spectrum_kernel, out_shape=(jax.ShapeDtypeStruct((4, WIN,...  82.1 us
    pallas_call x1, Pallas kernels, body(): pl.pallas_call(functools.partial(final_kernel, 1.0 / ((TM - 1) * energy))...  2.83 us
    unnamed x4, local copies, waits for them, and re-layouts  2.26 us

profile of v1, /device:TPU:105, one launch (start us, length us, event | category | flops | bytes accessed | tf_op | source)
XLA Modules:
  0.0 87.2 jit_solution(1207884051786736190)
XLA Ops:
  0.0 82.1 %shard_map.55 = (f32[4,64,1024]{2,1,0:T(8,128)}, bf16[4,64,1024]{2,1,0:T(8,128)(2,1)}) custom-call(bf16[32,64,1024]{2,1,0:T(8,128)(2,1)} %h_ref.1, bf16[2,512,512]{2,1,0:T(8,128)(2,1)} %constant.8.clone.ty_ref, bf16[512,1024]{1,0:T(8,128)(2,1)} %constant.9.clone.tx_ref, bf16[256,256]{1,0:T(8,128)(2,1)} %constant.10.clone.time_ref, ...), custom_call_target="tpu_custom_call" | custom-call | tf_op jit(solution)/shard_map/pallas_call | solution.py:352
  82.1 0.0 copy-start
  82.1 1.2 %copy-done = f32[4,64,1024]{2,1,0:T(8,128)S(1)} copy-done((f32[4,64,1024]{2,1,0:T(8,128)S(1)}, f32[4,64,1024]{2,1,0:T(8,128)}, u32[]{:S(2)}) %copy-start) | copy-done | bytes 1048600
  83.3 0.0 copy-start.1
  83.3 1.0 %copy-done.1 = bf16[4,64,1024]{2,1,0:T(8,128)(2,1)S(1)} copy-done((bf16[4,64,1024]{2,1,0:T(8,128)(2,1)S(1)}, bf16[4,64,1024]{2,1,0:T(8,128)(2,1)}, u32[]{:S(2)}) %copy-start.1) | copy-done | bytes 524312
  84.4 2.8 %shard_map.56 = f32[64,8,1024]{2,1,0:T(8,128)} custom-call(f32[256,1024]{1,0:T(8,128)S(1)} %bitcast.2, bf16[256,1024]{1,0:T(8,128)(2,1)S(1)} %bitcast.3), custom_call_target="tpu_custom_call" | custom-call | tf_op jit(solution)/shard_map/pallas_call | solution.py:388
Async XLA Ops:
  82.1 1.2 %copy-start = (f32[4,64,1024]{2,1,0:T(8,128)S(1)}, f32[4,64,1024]{2,1,0:T(8,128)}, u32[]{:S(2)}) copy-start(f32[4,64,1024]{2,1,0:T(8,128)} %get-tuple-element.7) | copy-start | bytes 3145732
  83.3 1.0 %copy-start.1 = (bf16[4,64,1024]{2,1,0:T(8,128)(2,1)S(1)}, bf16[4,64,1024]{2,1,0:T(8,128)(2,1)}, u32[]{:S(2)}) copy-start(bf16[4,64,1024]{2,1,0:T(8,128)(2,1)} %get-tuple-element.8) | copy-start | bytes 1572868

commit v2 on v1

--- a/solution.py
+++ b/solution.py
@@ -19,6 +19,7 @@
 DEVICES = TM * ROWS
 FRAMES_DEV = 32
 X_DEV = 64
+VMEM_ALL = 67_000_000
 BF16 = jnp.bfloat16
 F32 = jnp.float32
 
@@ -95,10 +96,15 @@
     return x * 2 + z // 2, (z % 2 * 4 + y) * 2 + core
 
 
+def far(step):
+    a, b = step // ROWS, step % ROWS
+    return min(a // 2, 4 - a // 2) + a % 2 * 2 + b // 8 + min(b // 2 % 4, 4 - b // 2 % 4)
+
+
 def spectrum_kernel(
-    h_ref, ty_ref, tx_ref, time_ref, time0_ref, own_ref, got_ref,
-    tab, txa, txb, rowsum, send, recv, lhs, rc, rs, modes, msg,
-    send_sem, recv_sem, local_sem, msg_send_sem, msg_recv_sem,
+    h_hbm, ty_hbm, tx_hbm, time_ref, time0_ref, own_hbm, got_ref,
+    h_ref, ty_ref, tx_ref, own_ref, tab, txa, txb, rowsum, send, recv, lhs, rc, rs, modes, msg,
+    send_sem, recv_sem, local_sem, msg_send_sem, msg_recv_sem, load_sem, own_sem,
 ):
     tm, rows = lax.axis_index("tm"), lax.axis_index("rows")
     me = tm * ROWS + rows
@@ -107,27 +113,41 @@
     def device(target):
         return {"tm": target // ROWS, "rows": target % ROWS}
 
+    loads = [
+        pltpu.make_async_copy(source, target, load_sem.at[i])
+        for i, (source, target) in enumerate(
+            ((ty_hbm, ty_ref), (h_hbm, h_ref), (tx_hbm, tx_ref))
+        )
+    ]
+    for load in loads:
+        load.start()
+
     barrier = pltpu.get_barrier_semaphore()
-
-    @pl.loop(1, DEVICES)
-    def _(step):
+    tm_of = [(tm + a) % TM for a in range(TM)]
+    rows_of = [(rows + b) % ROWS for b in range(ROWS)]
+    for step in sorted(range(1, DEVICES), key=far, reverse=True):
         pl.semaphore_signal(
-            barrier, inc=1, device_id=device((me + step) % DEVICES), device_id_type=MESH
+            barrier,
+            inc=1,
+            device_id={"tm": tm_of[step // ROWS], "rows": rows_of[step % ROWS]},
+            device_id_type=MESH,
         )
 
+    loads[0].wait()
     row_sign = jnp.where(lax.broadcasted_iota(jnp.int32, (HALF, 1), 0) % 2 == 0, 1.0, -1.0)
     for phase in range(2):
         tab[phase, :, :HALF] = ty_ref[phase]
         tab[phase, :, HALF:] = (ty_ref[phase].astype(F32) * row_sign).astype(BF16)
-    lane_sign = jnp.where(lax.broadcasted_iota(jnp.int32, (1, GRID), 1) % 2 == 0, 1.0, -1.0)
-    txa[:HALF] = tx_ref[...]
-    txa[HALF:] = (tx_ref[...].astype(F32) * lane_sign).astype(BF16)
-
-    @pl.loop(0, 8)
-    def _(block):
-        base = pl.multiple_of(block * 128, 128)
-        txb[pl.ds(base, 64)] = txa[pl.ds(base + 64, 64)]
-        txb[pl.ds(base + 64, 64)] = txa[pl.ds(base, 64)]
+    def column_tables():
+        lane_sign = jnp.where(lax.broadcasted_iota(jnp.int32, (1, GRID), 1) % 2 == 0, 1.0, -1.0)
+        txa[:HALF] = tx_ref[...]
+        txa[HALF:] = (tx_ref[...].astype(F32) * lane_sign).astype(BF16)
+
+        @pl.loop(0, 8)
+        def _(block):
+            base = pl.multiple_of(block * 128, 128)
+            txb[pl.ds(base, 64)] = txa[pl.ds(base + 64, 64)]
+            txb[pl.ds(base + 64, 64)] = txa[pl.ds(base, 64)]
 
     def row_phase(phase):
         for inner in range(2):
@@ -277,6 +297,10 @@
     mirror = DEVICES - 1 - me
     first_to = jnp.where(me == 0, 64, jnp.where(me < 64, DEVICES - me, mirror))
 
+    def own_copy(phase):
+        slots = pl.ds(2 * phase, 2)
+        return pltpu.make_async_copy(own_ref.at[slots], own_hbm.at[slots], own_sem.at[phase])
+
     def message(slot):
         return pltpu.make_async_remote_copy(
             src_ref=msg.at[slot],
@@ -287,11 +311,14 @@
             device_id_type=MESH,
         )
 
+    loads[1].wait()
     row_phase(0)
     pl.semaphore_wait(barrier, DEVICES - 1)
     start_sends(0)
     row_phase(1)
     start_sends(1)
+    loads[2].wait()
+    column_tables()
     for phase in range(2):
         pltpu.make_async_copy(
             send.at[phase, me // 2, me % 2], recv.at[phase, me], local_sem.at[phase]
@@ -301,13 +328,24 @@
         time_phase(phase)
         for low in range(2):
             message(2 * phase + low).start()
+        own_copy(phase).start()
     for phase in range(2):
         wait_all(phase, send_sem)
+    for phase in range(2):
+        own_copy(phase).wait()
     for slot in range(4):
         message(slot).wait()
 
 
-def final_kernel(scale, own_ref, got_ref, out_ref, stack, left, flip):
+def final_kernel(
+    scale, own_hbm, got_hbm, out_hbm, own_ref, got_ref, stack, left, flip, result, in_sem, out_sem
+):
+    loads = [
+        pltpu.make_async_copy(own_hbm, own_ref, in_sem.at[0]),
+        pltpu.make_async_copy(got_hbm, got_ref, in_sem.at[1]),
+    ]
+    for load in loads:
+        load.start()
     me = lax.axis_index("tm") * ROWS + lax.axis_index("rows")
     upper = me >= 64
     i = lax.broadcasted_iota(jnp.int32, (HALF, HALF), 0)
@@ -317,14 +355,18 @@
     come = lax.broadcasted_iota(jnp.int32, (HALF, 256), 1)
     w, row = to // 8, to % 8
     w_from = jnp.where(upper, (WIN - w) % WIN, w)
-    slot_own = jnp.where(upper, jnp.where((row >= 1) & (row <= 4), 4 - row, -1), jnp.where(row < 4, row, -1))
+    slot_own = jnp.where(
+        upper, jnp.where((row >= 1) & (row <= 4), 4 - row, -1), jnp.where(row < 4, row, -1)
+    )
     slot_got = jnp.where(
-        upper, jnp.where(row == 0, 0, jnp.where(row >= 5, 8 - row, -1)), jnp.where(row >= 4, row - 4, -1)
-    )
-    own_map = jnp.where((come // WIN == slot_own) & (come % WIN == w_from), 1.0, 0.0).astype(BF16)
+        upper,
+        jnp.where(row == 0, 0, jnp.where(row >= 5, 8 - row, -1)),
+        jnp.where(row >= 4, row - 4, -1),
+    )
+    own_map = jnp.where(come == slot_own * WIN + w_from, 1.0, 0.0).astype(BF16)
     left[:, :256] = own_map
     left[:, 256:512] = own_map
-    left[:, 512:] = jnp.where((come // WIN == slot_got) & (come % WIN == w_from), 1.0, 0.0).astype(BF16)
+    left[:, 512:] = jnp.where(come == slot_got * WIN + w_from, 1.0, 0.0).astype(BF16)
     swap = (lax.broadcasted_iota(jnp.int32, (256, HALF), 1) >= 1) & upper
 
     def place(at, a, b):
@@ -332,20 +374,31 @@
         other = jnp.where(swap, a, b).astype(BF16)
         stack[at, HALF:] = jnp.dot(other, flip[...], preferred_element_type=F32).astype(BF16)
 
+    loads[0].wait()
     a, b = own_ref[:, :HALF], own_ref[:, HALF:]
     a_top, b_top = a.astype(BF16).astype(F32), b.astype(BF16).astype(F32)
     place(slice(0, 256), a_top, b_top)
     place(slice(256, 512), a - a_top, b - b_top)
+    loads[1].wait()
     place(slice(512, 768), got_ref[:, :HALF].astype(F32), got_ref[:, HALF:].astype(F32))
 
+    stores = []
     for part in range(4):
         columns = slice(part * 256, part * 256 + 256)
-        result = jnp.dot(left[...], stack[:, columns], preferred_element_type=F32) * scale
-        out_ref[:, :, columns] = result.reshape(WIN, 8, 256)
+        product = jnp.dot(left[...], stack[:, columns], preferred_element_type=F32) * scale
+        result[part] = product.reshape(WIN, 8, 256)
+        store = pltpu.make_async_copy(
+            result.at[part], out_hbm.at[:, :, pl.ds(part * 256, 256)], out_sem.at[part]
+        )
+        store.start()
+        stores.append(store)
+    for store in stores:
+        store.wait()
 
 
 def body(heights):
     vmem = pl.BlockSpec(memory_space=pltpu.VMEM)
+    hbm = pl.BlockSpec(memory_space=pl.ANY)
     time_matrix, time_first = time_matrices()
     energy = tapers()[2]
     dma = pltpu.SemaphoreType.DMA
@@ -355,9 +408,13 @@
             jax.ShapeDtypeStruct((4, WIN, GRID), F32),
             jax.ShapeDtypeStruct((4, WIN, GRID), BF16),
         ),
-        in_specs=[vmem] * 5,
-        out_specs=(vmem, vmem),
+        in_specs=[hbm] * 3 + [vmem] * 2,
+        out_specs=(hbm, hbm),
         scratch_shapes=[
+            pltpu.VMEM((FRAMES_DEV, X_DEV, GRID), BF16),
+            pltpu.VMEM((2, HALF, HALF), BF16),
+            pltpu.VMEM((HALF, GRID), BF16),
+            pltpu.VMEM((4, WIN, GRID), F32),
             pltpu.VMEM((2, HALF, GRID), BF16),
             pltpu.VMEM((GRID, GRID), BF16),
             pltpu.VMEM((GRID, GRID), BF16),
@@ -374,9 +431,11 @@
             dma((2,)),
             dma((4,)),
             dma((4,)),
+            dma((3,)),
+            dma((2,)),
         ],
         compiler_params=pltpu.CompilerParams(
-            collective_id=0, has_side_effects=True, vmem_limit_bytes=60 << 20
+            collective_id=0, has_side_effects=True, vmem_limit_bytes=VMEM_ALL
         ),
     )(
         heights,
@@ -388,14 +447,19 @@
     return pl.pallas_call(
         functools.partial(final_kernel, 1.0 / ((TM - 1) * energy)),
         out_shape=jax.ShapeDtypeStruct((WIN, 8, GRID), F32),
-        in_specs=[vmem, vmem],
-        out_specs=vmem,
+        in_specs=[hbm, hbm],
+        out_specs=hbm,
         scratch_shapes=[
+            pltpu.VMEM((256, GRID), F32),
+            pltpu.VMEM((256, GRID), BF16),
             pltpu.VMEM((768, GRID), BF16),
             pltpu.VMEM((HALF, 768), BF16),
             pltpu.VMEM((HALF, HALF), BF16),
+            pltpu.VMEM((4, WIN, 8, 256), F32),
+            dma((2,)),
+            dma((4,)),
         ],
-        compiler_params=pltpu.CompilerParams(vmem_limit_bytes=40 << 20),
+        compiler_params=pltpu.CompilerParams(vmem_limit_bytes=VMEM_ALL),
     )(own.reshape(256, GRID), got.reshape(256, GRID))
 
 

time: 87.4 us -> 82.4 us (0.943)
  Pallas kernels: 84.9 us -> 82.2 us
  local copies, waits for them, and re-layouts: 2.26 us -> 0 us
    pallas_call x1, Pallas kernels: 82.1 us -> 78.4 us  [body(): pl.pallas_call(spectrum_kernel, out_shape=(jax.ShapeDtypeStruct((4, WIN,...]
    unnamed x4 -> x0, local copies, waits for them, and re-layouts: 2.26 us -> none
    pallas_call x1, Pallas kernels: 2.83 us -> 3.81 us  [body(): pl.pallas_call(functools.partial(final_kernel, 1.0 / ((TM - 1) * energy))...]
where the time goes in v2:
time: 82.4 us; the launch traced here: 82.2 us
  Pallas kernels  82.2 us (100%)
    pallas_call x1, Pallas kernels, body(): pl.pallas_call(spectrum_kernel, out_shape=(jax.ShapeDtypeStruct((4, WIN,...  78.4 us
    pallas_call x1, Pallas kernels, body(): pl.pallas_call(functools.partial(final_kernel, 1.0 / ((TM - 1) * energy))...  3.81 us

profile of v2, /device:TPU:105, one launch (start us, length us, event | category | flops | bytes accessed | tf_op | source)
XLA Modules:
  0.0 82.2 jit_solution(1472609613508929862)
XLA Ops:
  0.0 78.4 %shard_map.55 = (f32[4,64,1024]{2,1,0:T(8,128)}, bf16[4,64,1024]{2,1,0:T(8,128)(2,1)}) custom-call(bf16[32,64,1024]{2,1,0:T(8,128)(2,1)} %h_hbm.1, bf16[2,512,512]{2,1,0:T(8,128)(2,1)} %constant.8.clone.ty_hbm, bf16[512,1024]{1,0:T(8,128)(2,1)} %constant.9.clone.tx_hbm, bf16[256,256]{1,0:T(8,128)(2,1)} %constant.10.clone.time_ref, ...), custom_call_target="tpu_custom_call" | custom-call | tf_op jit(solution)/shard_map/pallas_call | solution.py:405
  78.4 3.8 %shard_map.56 = f32[64,8,1024]{2,1,0:T(8,128)} custom-call(f32[256,1024]{1,0:T(8,128)} %bitcast.2, bf16[256,1024]{1,0:T(8,128)(2,1)} %bitcast.3), custom_call_target="tpu_custom_call" | custom-call | tf_op jit(solution)/shard_map/pallas_call | solution.py:447

commit v3 on v2

v3 whole, which is shorter than its diff:
```python
import functools
import math

import jax
import jax.numpy as jnp
import ml_dtypes
import numpy as np
from jax import lax
from jax.experimental import pallas as pl
from jax.experimental.pallas import tpu as pltpu
from jax.sharding import PartitionSpec as P

MESH = pl.DeviceIdType.MESH
GRID = 1024
HALF = 512
WIN = 64
TM = 8
ROWS = 16
DEVICES = TM * ROWS
FRAMES_DEV = 32
X_DEV = 64
SLOTS = 4
QUARTER = 256
VMEM_ALL = 67_000_000
BF16 = jnp.bfloat16
F32 = jnp.float32


def trig(index):
    angles = (index % GRID).astype(np.float32) * np.float32(2.0 * math.pi / GRID)
    scale = np.float32(math.sqrt(GRID))
    return np.cos(angles) / scale, np.sin(angles) / scale


def row_table():
    row = np.arange(QUARTER)
    quad, part, low = row // 8, row // 4 % 2, row % 4
    device = 4 * quad + low
    y = np.arange(HALF)
    tables = []
    for slot in range(SLOTS):
        q = np.where(device < 64, 8 * device + slot, 8 * (127 - device) + 4 + slot)
        cosine, sine = trig(q[:, None] * y[None, :])
        values = np.where(part[:, None] == 0, cosine, -sine)
        shared = (device == 0) & (slot == 0) & (part == 1)
        nyquist, _ = trig(HALF * y)
        tables.append(np.where(shared[:, None], nyquist[None, :], values))
    return np.stack(tables).astype(ml_dtypes.bfloat16)


def column_table():
    x = np.arange(HALF)
    cosine, sine = trig(x[:, None] * x[None, :])
    sine[:, 0] = trig(x * HALF)[0]
    return np.concatenate([cosine, sine], 1).astype(ml_dtypes.bfloat16)


def tapers():
    t = np.arange(WIN)
    hann = np.float32(0.5) - np.float32(0.5) * np.cos(
        t.astype(np.float32) * np.float32(2.0 * math.pi / WIN)
    )
    angles = (t[:, None] * t[None, :] % WIN).astype(np.float32) * np.float32(2.0 * math.pi / WIN)
    energy = float(np.sum(hann * hann, dtype=np.float32))

    def rounded(values):
        return (values * hann[None, :]).astype(ml_dtypes.bfloat16).astype(np.float32)

    return rounded(np.cos(angles)), rounded(np.sin(angles)), energy


def time_matrices():
    cosine, sine, _ = tapers()
    k = np.arange(128)
    block, second, inner = k // 64, k // 32 % 2, k // 16 % 2
    high, part, low = k // 8 % 2, k // 4 % 2, k % 4
    t = 32 * block + 16 * high + 4 * low + 2 * inner + second
    real = np.where(part == 0, cosine[:, t], sine[:, t])
    imag = np.where(part == 0, -sine[:, t], cosine[:, t])
    back = (-np.arange(WIN)) % WIN
    return np.concatenate([real, imag, real[back], imag[back]]).astype(ml_dtypes.bfloat16)


def far(step):
    a, b = step // ROWS, step % ROWS
    return min(a // 2, 4 - a // 2) + a % 2 * 2 + b // 8 + min(b // 2 % 4, 4 - b // 2 % 4)


def spectrum_kernel(
    h_hbm, ty_hbm, tx_hbm, time_ref, own_hbm, got_hbm,
    h_ref, ty_ref, tx_ref, own_ref, tab, txa, txb, rowsum, send, recv, lhs, rc, rs, modes, msg,
    send_sem, recv_sem, local_sem, msg_send_sem, msg_recv_sem, load_sem, own_sem,
):
    tm, rows = lax.axis_index("tm"), lax.axis_index("rows")
    me = tm * ROWS + rows
    x, y, z, core = tm // 2, rows // 2 % 4, tm % 2 * 2 + rows // 8, rows % 2

    loads = [
        pltpu.make_async_copy(source, target, load_sem.at[i])
        for i, (source, target) in enumerate(
            ((ty_hbm, ty_ref), (h_hbm, h_ref), (tx_hbm, tx_ref))
        )
    ]
    for load in loads:
        load.start()

    barrier = pltpu.get_barrier_semaphore()
    tm_of = [(tm + a) % TM for a in range(TM)]
    rows_of = [(rows + b) % ROWS for b in range(ROWS)]
    for step in sorted(range(1, DEVICES), key=far, reverse=True):
        pl.semaphore_signal(
            barrier,
            inc=1,
            device_id={"tm": tm_of[step // ROWS], "rows": rows_of[step % ROWS]},
            device_id_type=MESH,
        )

    def row_tables(slot):
        tab[slot, :, :HALF] = ty_ref[slot]
        tab[slot, :, HALF:] = -ty_ref[slot] if slot % 2 else ty_ref[slot]

    def column_tables():
        lane_sign = jnp.where(lax.broadcasted_iota(jnp.int32, (1, GRID), 1) % 2 == 0, 1.0, -1.0)
        txa[:HALF] = tx_ref[...]
        txa[HALF:] = (tx_ref[...].astype(F32) * lane_sign).astype(BF16)

        @pl.loop(0, 8)
        def _(block):
            base = pl.multiple_of(block * 128, 128)
            txb[pl.ds(base, 64)] = txa[pl.ds(base + 64, 64)]
            txb[pl.ds(base + 64, 64)] = txa[pl.ds(base, 64)]

    def row_phase(slot):
        @pl.loop(0, 8)
        def _(eighth):
            base = eighth * 4
            block = jnp.concatenate(
                [
                    h_ref[base + core],
                    h_ref[base + 1 - core],
                    h_ref[base + 2 + core],
                    h_ref[base + 3 - core],
                ],
                0,
            )
            rowsum[eighth] = lax.dot_general(
                tab[slot], block, (((1,), (1,)), ((), ())), preferred_element_type=F32
            )

        @pl.loop(0, 8)
        def _(part):
            at = pl.ds(pl.multiple_of(part * 32, 32), 32)
            row = lax.broadcasted_iota(jnp.int32, (4, 8, 256), 1)
            pair, single = row // 2 % 2 == 0, row % 2 == 0
            halves = []
            for high in range(2):
                r = [rowsum[4 * high + f, at].reshape(4, 8, 256) for f in range(4)]
                a = [None] * 4
                for f in range(2):
                    a[f] = jnp.where(pair, r[f], pltpu.roll(r[f + 2], 2, 1))
                    a[f + 2] = jnp.where(pair, pltpu.roll(r[f], 6, 1), r[f + 2])
                halves.append(
                    [
                        jnp.where(single, a[0], pltpu.roll(a[1], 1, 1)),
                        jnp.where(single, pltpu.roll(a[0], 7, 1), a[1]),
                        jnp.where(single, a[2], pltpu.roll(a[3], 1, 1)),
                        jnp.where(single, pltpu.roll(a[2], 7, 1), a[3]),
                    ]
                )
            for low in range(4):
                send[slot, pl.ds(part * 4, 4), low] = jnp.concatenate(
                    [halves[0][low], halves[1][low]], 1
                ).astype(BF16)

    def start_sends(slot):
        y_of = [(y + d) % 4 * 2 for d in range(4)]
        z_of = [(z + d) % 4 for d in range(4)]
        z_tm, z_rows = [v // 2 for v in z_of], [v % 2 * 8 for v in z_of]
        core_of = [core, 1 - core]

        @pl.loop(0, 4)
        def _(turn):
            x_of = [(x + 3 * turn + d) % 4 * 2 for d in range(4)]

            def start(step):
                shift = step * 91 % DEVICES
                to_tm = x_of[shift // 32] + z_tm[shift // 2 % 4]
                to_rows = z_rows[shift // 2 % 4] + y_of[shift // 8 % 4] + core_of[shift % 2]
                target = to_tm * ROWS + to_rows
                pltpu.make_async_remote_copy(
                    src_ref=send.at[slot, target // 4, target % 4],
                    dst_ref=recv.at[slot, me],
                    send_sem=send_sem.at[slot],
                    recv_sem=recv_sem.at[slot],
                    device_id={"tm": to_tm, "rows": to_rows},
                    device_id_type=MESH,
                ).start()

            @pl.when(turn > 0)
            def _():
                start(0)

            for step in range(1, 32):
                start(step)

        local_copy(slot).start()

    def local_copy(slot):
        return pltpu.make_async_copy(
            send.at[slot, me // 4, me % 4], recv.at[slot, me], local_sem.at[slot]
        )

    def wait_all(slot, sem):
        blocks = recv.at[slot, pl.ds(0, DEVICES - 1)]
        pltpu.make_async_copy(blocks, blocks, sem.at[slot]).wait()

    def gather_phase(slot):
        @pl.loop(0, TM)
        def _(block):
            low = lax.broadcasted_iota(jnp.int32, (16, 256), 1) % 128 < 64
            for pair in range(8):
                even = recv[slot, block * ROWS + 2 * pair]
                odd = recv[slot, block * ROWS + 2 * pair + 1]
                first = jnp.where(low, even, odd)
                second = jnp.where(low, odd, even)
                for inner in range(2):
                    at = pl.ds(pl.multiple_of(block * 32 + inner * 16, 16), 16)
                    lanes = slice(inner * 128, inner * 128 + 128)
                    columns = slice(pair * 128, pair * 128 + 128)
                    lhs[0, at, columns] = first[:, lanes]
                    lhs[1, at, columns] = second[:, lanes]

    def column_phase(part):
        columns = slice(part * 256, part * 256 + 256)
        above = slice(HALF + part * 256, HALF + part * 256 + 256)
        for second in range(2):
            table = txb if second else txa
            rc[...] = jnp.dot(lhs[second], table[:, columns], preferred_element_type=F32)
            rs[...] = jnp.dot(lhs[second], table[:, above], preferred_element_type=F32)

            @pl.loop(0, TM)
            def _(block):
                at = pl.ds(pl.multiple_of(block * 32, 32), 32)
                cosine = rc[at].reshape(4, 8, 256)
                sine = rs[at].reshape(4, 8, 256)
                top = lax.broadcasted_iota(jnp.int32, (4, 8, 256), 1) < 4
                swapped = pltpu.roll(sine, 4, 1)
                swapped = jnp.where(top, swapped, -swapped)
                plus, minus = cosine + swapped, cosine - swapped
                if part == 0:
                    edge = lax.broadcasted_iota(jnp.int32, (4, 8, 256), 2) == 0
                    plus = jnp.where(edge, cosine, plus)
                    minus = jnp.where(edge, sine, minus)
                modes[block, second, :, columns] = plus.reshape(32, 256).astype(BF16)
                modes[block, second, :, above] = minus.reshape(32, 256).astype(BF16)

    def window_at(window, columns):
        return modes[pl.ds(window, 2), :, :, columns].reshape(128, 256)

    def time_phase(slot, part):
        for half in range(2):
            columns = slice(half * HALF + part * 256, half * HALF + part * 256 + 256)
            total = None
            for window in range(TM - 1):
                u = jnp.dot(
                    time_ref[:128], window_at(window, columns), preferred_element_type=F32
                )
                u = u * u
                power = u[:64] + u[64:]
                total = power if total is None else total + power
            own_ref[slot, :, columns] = total
            msg[slot, part, :, half * 256 : half * 256 + 256] = total.astype(BF16)

        @pl.when((me == 0) & (slot == 0))
        def _():
            columns = slice(part * 256, part * 256 + 256)
            above = slice(HALF + part * 256, HALF + part * 256 + 256)
            lane = lax.broadcasted_iota(jnp.int32, (128, 256), 1) + part * 256
            sums = [None] * 4
            for window in range(TM - 1):
                a, b = (
                    jnp.dot(time_ref[...], window_at(window, at), preferred_element_type=F32)
                    for at in (columns, above)
                )
                back_a = jnp.where(lane == 0, a[128:], b[128:])
                back_b = jnp.where(lane == 0, b[128:], a[128:])
                terms = []
                for here, back in ((a[:128], back_a), (b[:128], back_b)):
                    r, i, rb, ib = here[:64], here[64:], back[:64], back[64:]
                    terms.append((r + rb) * (r + rb) + (i - ib) * (i - ib))
                    terms.append((r - rb) * (r - rb) + (i + ib) * (i + ib))
                sums = [t if s is None else s + t for s, t in zip(sums, terms)]
            own_ref[0, :, columns] = sums[0] * 0.25
            own_ref[0, :, above] = sums[2] * 0.25
            msg[0, part, :, :256] = (sums[1] * 0.25).astype(BF16)
            msg[0, part, :, 256:] = (sums[3] * 0.25).astype(BF16)

    def own_copy(slot):
        return pltpu.make_async_copy(own_ref.at[slot], own_hbm.at[slot], own_sem.at[slot])

    mirror = DEVICES - 1 - me
    first_to = jnp.where(me == 0, 64, jnp.where(me < 64, DEVICES - me, mirror))

    def message(slot, part):
        target = jnp.where(slot == 0, first_to, mirror)
        return pltpu.make_async_remote_copy(
            src_ref=msg.at[slot, part],
            dst_ref=got_hbm.at[slot, part],
            send_sem=msg_send_sem.at[slot, part],
            recv_sem=msg_recv_sem.at[slot, part],
            device_id={"tm": target // ROWS, "rows": target % ROWS},
            device_id_type=MESH,
        )

    loads[0].wait()
    row_tables(0)
    loads[1].wait()
    row_phase(0)
    pl.semaphore_wait(barrier, DEVICES - 1)
    for slot in range(1, SLOTS):
        row_tables(slot)

    @pl.loop(0, SLOTS)
    def _(slot):
        start_sends(slot)

        @pl.when(slot < SLOTS - 1)
        def _():
            row_phase(slot + 1)

    loads[2].wait()
    column_tables()

    @pl.loop(0, SLOTS)
    def _(slot):
        local_copy(slot).wait()
        wait_all(slot, recv_sem)
        gather_phase(slot)
        for part in range(2):
            column_phase(part)
            time_phase(slot, part)
            message(slot, part).start()
        own_copy(slot).start()

    @pl.loop(0, SLOTS)
    def _(slot):
        wait_all(slot, send_sem)
        own_copy(slot).wait()
        for part in range(2):
            message(slot, part).wait()


def final_kernel(
    scale, own_hbm, got_hbm, out_hbm, own_ref, got_ref, stack, left, flip, result, in_sem, out_sem
):
    loads = [
        pltpu.make_async_copy(own_hbm, own_ref, in_sem.at[0]),
        pltpu.make_async_copy(got_hbm, got_ref, in_sem.at[1]),
    ]
    for load in loads:
        load.start()
    me = lax.axis_index("tm") * ROWS + lax.axis_index("rows")
    upper = me >= 64
    i = lax.broadcasted_iota(jnp.int32, (HALF, HALF), 0)
    j = lax.broadcasted_iota(jnp.int32, (HALF, HALF), 1)
    flip[...] = jnp.where(i == (HALF - j) % HALF, 1.0, 0.0).astype(BF16)
    to = lax.broadcasted_iota(jnp.int32, (HALF, 256), 0)
    come = lax.broadcasted_iota(jnp.int32, (HALF, 256), 1)
    w, row = to // 8, to % 8
    w_from = jnp.where(upper, (WIN - w) % WIN, w)
    slot_own = jnp.where(
        upper, jnp.where((row >= 1) & (row <= 4), 4 - row, -1), jnp.where(row < 4, row, -1)
    )
    slot_got = jnp.where(
        upper,
        jnp.where(row == 0, 0, jnp.where(row >= 5, 8 - row, -1)),
        jnp.where(row >= 4, row - 4, -1),
    )
    own_map = jnp.where(come == slot_own * WIN + w_from, 1.0, 0.0).astype(BF16)
    left[:, :256] = own_map
    left[:, 256:512] = own_map
    left[:, 512:] = jnp.where(come == slot_got * WIN + w_from, 1.0, 0.0).astype(BF16)
    swap = (lax.broadcasted_iota(jnp.int32, (256, HALF), 1) >= 1) & upper

    def place(at, a, b):
        stack[at, :HALF] = jnp.where(swap, b, a).astype(BF16)
        other = jnp.where(swap, a, b).astype(BF16)
        stack[at, HALF:] = jnp.dot(other, flip[...], preferred_element_type=F32).astype(BF16)

    loads[0].wait()
    a, b = own_ref[:, :HALF], own_ref[:, HALF:]
    a_top, b_top = a.astype(BF16).astype(F32), b.astype(BF16).astype(F32)
    place(slice(0, 256), a_top, b_top)
    place(slice(256, 512), a - a_top, b - b_top)
    loads[1].wait()
    halves = [
        jnp.concatenate(
            [got_ref[:, part, :, at].reshape(256, 256).astype(F32) for part in range(2)], 1
        )
        for at in (slice(0, 256), slice(256, 512))
    ]
    place(slice(512, 768), *halves)

    stores = []
    for part in range(4):
        columns = slice(part * 256, part * 256 + 256)
        product = jnp.dot(left[...], stack[:, columns], preferred_element_type=F32) * scale
        result[part] = product.reshape(WIN, 8, 256)
        store = pltpu.make_async_copy(
            result.at[part], out_hbm.at[:, :, pl.ds(part * 256, 256)], out_sem.at[part]
        )
        store.start()
        stores.append(store)
    for store in stores:
        store.wait()


def body(heights):
    vmem = pl.BlockSpec(memory_space=pltpu.VMEM)
    hbm = pl.BlockSpec(memory_space=pl.ANY)
    energy = tapers()[2]
    dma = pltpu.SemaphoreType.DMA
    own, got = pl.pallas_call(
        spectrum_kernel,
        out_shape=(
            jax.ShapeDtypeStruct((SLOTS, WIN, GRID), F32),
            jax.ShapeDtypeStruct((SLOTS, 2, WIN, HALF), BF16),
        ),
        in_specs=[hbm] * 3 + [vmem],
        out_specs=(hbm, hbm),
        scratch_shapes=[
            pltpu.VMEM((FRAMES_DEV, X_DEV, GRID), BF16),
            pltpu.VMEM((SLOTS, QUARTER, HALF), BF16),
            pltpu.VMEM((HALF, GRID), BF16),
            pltpu.VMEM((SLOTS, WIN, GRID), F32),
            pltpu.VMEM((SLOTS, QUARTER, GRID), BF16),
            pltpu.VMEM((GRID, GRID), BF16),
            pltpu.VMEM((GRID, GRID), BF16),
            pltpu.VMEM((8, QUARTER, 256), F32),
            pltpu.VMEM((SLOTS, DEVICES // 4, 4, 16, 256), BF16),
            pltpu.VMEM((SLOTS, DEVICES, 16, 256), BF16),
            pltpu.VMEM((2, QUARTER, GRID), BF16),
            pltpu.VMEM((QUARTER, 256), F32),
            pltpu.VMEM((QUARTER, 256), F32),
            pltpu.VMEM((TM, 2, 32, GRID), BF16),
            pltpu.VMEM((SLOTS, 2, WIN, HALF), BF16),
            dma((SLOTS,)),
            dma((SLOTS,)),
            dma((SLOTS,)),
            dma((SLOTS, 2)),
            dma((SLOTS, 2)),
            dma((3,)),
            dma((SLOTS,)),
        ],
        compiler_params=pltpu.CompilerParams(
            collective_id=0, has_side_effects=True, vmem_limit_bytes=VMEM_ALL
        ),
    )(
        heights,
        jnp.asarray(row_table()),
        jnp.asarray(column_table()),
        jnp.asarray(time_matrices()),
    )
    return pl.pallas_call(
        functools.partial(final_kernel, 1.0 / ((TM - 1) * energy)),
        out_shape=jax.ShapeDtypeStruct((WIN, 8, GRID), F32),
        in_specs=[hbm, hbm],
        out_specs=hbm,
        scratch_shapes=[
            pltpu.VMEM((256, GRID), F32),
            pltpu.VMEM((SLOTS, 2, WIN, HALF), BF16),
            pltpu.VMEM((768, GRID), BF16),
            pltpu.VMEM((HALF, 768), BF16),
            pltpu.VMEM((HALF, HALF), BF16),
            pltpu.VMEM((4, WIN, 8, 256), F32),
            dma((2,)),
            dma((4,)),
        ],
        compiler_params=pltpu.CompilerParams(vmem_limit_bytes=VMEM_ALL),
    )(own.reshape(256, GRID), got)


def solution(mesh):
    return jax.shard_map(
        body,
        mesh=mesh,
        in_specs=(P("tm", "rows", None),),
        out_specs=P(None, ("tm", "rows"), None),
        check_vma=False,
    )
```

time: 82.4 us -> 80 us (0.971)
  the two profiles are of different devices: /device:TPU:105 before, /device:TPU:69 now
where the time goes in v3:
time: 80 us; the launch traced here: 78.4 us
  Pallas kernels  78.4 us (98%)
    pallas_call x1, Pallas kernels, body(): pl.pallas_call(spectrum_kernel, out_shape=(jax.ShapeDtypeStruct((SLOTS, W...  74.6 us
    pallas_call x1, Pallas kernels, body(): pl.pallas_call(functools.partial(final_kernel, 1.0 / ((TM - 1) * energy))...  3.81 us

profile of v3, /device:TPU:69, one launch (start us, length us, event | category | flops | bytes accessed | tf_op | source)
XLA Modules:
  0.0 78.4 jit_solution(12691926352237702359)
XLA Ops:
  0.0 74.6 %shard_map.46 = (f32[4,64,1024]{2,1,0:T(8,128)}, bf16[4,2,64,512]{3,2,1,0:T(8,128)(2,1)}) custom-call(bf16[32,64,1024]{2,1,0:T(8,128)(2,1)} %h_hbm.1, bf16[4,256,512]{2,1,0:T(8,128)(2,1)} %constant.6.clone.ty_hbm, bf16[512,1024]{1,0:T(8,128)(2,1)} %constant.7.clone.tx_hbm, bf16[256,128]{1,0:T(8,128)(2,1)} %constant.8.clone.time_ref), custom_call_target="tpu_custom_call" | custom-call | tf_op jit(solution)/shard_map/pallas_call | solution.py:423
  74.6 3.8 %shard_map.47 = f32[64,8,1024]{2,1,0:T(8,128)} custom-call(f32[256,1024]{1,0:T(8,128)} %bitcast.1, bf16[4,2,64,512]{3,2,1,0:T(8,128)(2,1)} %get-tuple-element.8.got_hbm), custom_call_target="tpu_custom_call" | custom-call | tf_op jit(solution)/shard_map/pallas_call | solution.py:464

commit v4 on v3

--- a/solution.py
+++ b/solution.py
@@ -86,23 +86,36 @@
     return min(a // 2, 4 - a // 2) + a % 2 * 2 + b // 8 + min(b // 2 % 4, 4 - b // 2 % 4)
 
 
+def make_flip(flip):
+    i = lax.broadcasted_iota(jnp.int32, (HALF, HALF), 0)
+    j = lax.broadcasted_iota(jnp.int32, (HALF, HALF), 1)
+    flip[...] = jnp.where(i == (HALF - j) % HALF, 1.0, 0.0).astype(BF16)
+
+
 def spectrum_kernel(
     h_hbm, ty_hbm, tx_hbm, time_ref, own_hbm, got_hbm,
-    h_ref, ty_ref, tx_ref, own_ref, tab, txa, txb, rowsum, send, recv, lhs, rc, rs, modes, msg,
-    send_sem, recv_sem, local_sem, msg_send_sem, msg_recv_sem, load_sem, own_sem,
+    h_ref, ty_ref, tx_ref, own_ref, tab, txa, txb, rowsum, send, recv, lhs, rc, rs, modes, msg, stack, flip,
+    send_sem, recv_sem, local_sem, msg_send_sem, msg_recv_sem, load_sem, height_sem, own_sem,
 ):
     tm, rows = lax.axis_index("tm"), lax.axis_index("rows")
     me = tm * ROWS + rows
     x, y, z, core = tm // 2, rows // 2 % 4, tm % 2 * 2 + rows // 8, rows % 2
 
+    def height_load(eighth):
+        frames = pl.ds(eighth * 4, 4)
+        return pltpu.make_async_copy(h_hbm.at[frames], h_ref.at[frames], height_sem.at[eighth])
+
+    later = pl.ds(1, SLOTS - 1)
     loads = [
-        pltpu.make_async_copy(source, target, load_sem.at[i])
-        for i, (source, target) in enumerate(
-            ((ty_hbm, ty_ref), (h_hbm, h_ref), (tx_hbm, tx_ref))
-        )
+        pltpu.make_async_copy(ty_hbm.at[0], ty_ref.at[0], load_sem.at[0]),
+        pltpu.make_async_copy(ty_hbm.at[later], ty_ref.at[later], load_sem.at[1]),
+        pltpu.make_async_copy(tx_hbm, tx_ref, load_sem.at[2]),
     ]
-    for load in loads:
-        load.start()
+    loads[0].start()
+    for eighth in range(8):
+        height_load(eighth).start()
+    loads[1].start()
+    loads[2].start()
 
     barrier = pltpu.get_barrier_semaphore()
     tm_of = [(tm + a) % TM for a in range(TM)]
@@ -131,8 +144,12 @@
             txb[pl.ds(base + 64, 64)] = txa[pl.ds(base, 64)]
 
     def row_phase(slot):
+        first = isinstance(slot, int)
+
         @pl.loop(0, 8)
         def _(eighth):
+            if first:
+                height_load(eighth).wait()
             base = eighth * 4
             block = jnp.concatenate(
                 [
@@ -295,8 +312,20 @@
             msg[0, part, :, :256] = (sums[1] * 0.25).astype(BF16)
             msg[0, part, :, 256:] = (sums[3] * 0.25).astype(BF16)
 
+    def own_phase(slot):
+        swap = (lax.broadcasted_iota(jnp.int32, (WIN, HALF), 1) >= 1) & (me >= 64)
+        a, b = own_ref[slot, :, :HALF], own_ref[slot, :, HALF:]
+        a, b = jnp.where(swap, b, a), jnp.where(swap, a, b)
+        a_top, b_top = a.astype(BF16), b.astype(BF16)
+        stack[slot, 0, :, :HALF] = a_top
+        stack[slot, 1, :, :HALF] = (a - a_top.astype(F32)).astype(BF16)
+        falling = jnp.concatenate([b_top, (b - b_top.astype(F32)).astype(BF16)], 0)
+        falling = jnp.dot(falling, flip[...], preferred_element_type=F32).astype(BF16)
+        stack[slot, 0, :, HALF:] = falling[:WIN]
+        stack[slot, 1, :, HALF:] = falling[WIN:]
+
     def own_copy(slot):
-        return pltpu.make_async_copy(own_ref.at[slot], own_hbm.at[slot], own_sem.at[slot])
+        return pltpu.make_async_copy(stack.at[slot], own_hbm.at[slot], own_sem.at[slot])
 
     mirror = DEVICES - 1 - me
     first_to = jnp.where(me == 0, 64, jnp.where(me < 64, DEVICES - me, mirror))
@@ -314,9 +343,9 @@
 
     loads[0].wait()
     row_tables(0)
-    loads[1].wait()
     row_phase(0)
     pl.semaphore_wait(barrier, DEVICES - 1)
+    loads[1].wait()
     for slot in range(1, SLOTS):
         row_tables(slot)
 
@@ -330,6 +359,7 @@
 
     loads[2].wait()
     column_tables()
+    make_flip(flip)
 
     @pl.loop(0, SLOTS)
     def _(slot):
@@ -340,6 +370,7 @@
             column_phase(part)
             time_phase(slot, part)
             message(slot, part).start()
+        own_phase(slot)
         own_copy(slot).start()
 
     @pl.loop(0, SLOTS)
@@ -351,21 +382,19 @@
 
 
 def final_kernel(
-    scale, own_hbm, got_hbm, out_hbm, own_ref, got_ref, stack, left, flip, result, in_sem, out_sem
+    scale, own_hbm, got_hbm, out_hbm, stack, got_ref, left, flip, result, in_sem, out_sem
 ):
     loads = [
-        pltpu.make_async_copy(own_hbm, own_ref, in_sem.at[0]),
-        pltpu.make_async_copy(got_hbm, got_ref, in_sem.at[1]),
+        pltpu.make_async_copy(got_hbm, got_ref, in_sem.at[0]),
+        pltpu.make_async_copy(own_hbm, stack.at[pl.ds(0, HALF)], in_sem.at[1]),
     ]
     for load in loads:
         load.start()
     me = lax.axis_index("tm") * ROWS + lax.axis_index("rows")
     upper = me >= 64
-    i = lax.broadcasted_iota(jnp.int32, (HALF, HALF), 0)
-    j = lax.broadcasted_iota(jnp.int32, (HALF, HALF), 1)
-    flip[...] = jnp.where(i == (HALF - j) % HALF, 1.0, 0.0).astype(BF16)
-    to = lax.broadcasted_iota(jnp.int32, (HALF, 256), 0)
-    come = lax.broadcasted_iota(jnp.int32, (HALF, 256), 1)
+    make_flip(flip)
+    to = lax.broadcasted_iota(jnp.int32, (HALF, HALF), 0)
+    come = lax.broadcasted_iota(jnp.int32, (HALF, HALF), 1)
     w, row = to // 8, to % 8
     w_from = jnp.where(upper, (WIN - w) % WIN, w)
     slot_own = jnp.where(
@@ -376,30 +405,24 @@
         jnp.where(row == 0, 0, jnp.where(row >= 5, 8 - row, -1)),
         jnp.where(row >= 4, row - 4, -1),
     )
-    own_map = jnp.where(come == slot_own * WIN + w_from, 1.0, 0.0).astype(BF16)
-    left[:, :256] = own_map
-    left[:, 256:512] = own_map
-    left[:, 512:] = jnp.where(come == slot_got * WIN + w_from, 1.0, 0.0).astype(BF16)
+    from_own = (come // 128 == slot_own) & (come % WIN == w_from)
+    from_got = come == slot_got * WIN + w_from
+    left[:, :HALF] = jnp.where(from_own, 1.0, 0.0).astype(BF16)
+    left[:, HALF:] = jnp.where(from_got, 1.0, 0.0)[:, :256].astype(BF16)
     swap = (lax.broadcasted_iota(jnp.int32, (256, HALF), 1) >= 1) & upper
 
-    def place(at, a, b):
-        stack[at, :HALF] = jnp.where(swap, b, a).astype(BF16)
-        other = jnp.where(swap, a, b).astype(BF16)
-        stack[at, HALF:] = jnp.dot(other, flip[...], preferred_element_type=F32).astype(BF16)
-
     loads[0].wait()
-    a, b = own_ref[:, :HALF], own_ref[:, HALF:]
-    a_top, b_top = a.astype(BF16).astype(F32), b.astype(BF16).astype(F32)
-    place(slice(0, 256), a_top, b_top)
-    place(slice(256, 512), a - a_top, b - b_top)
-    loads[1].wait()
-    halves = [
+    a, b = (
         jnp.concatenate(
             [got_ref[:, part, :, at].reshape(256, 256).astype(F32) for part in range(2)], 1
         )
         for at in (slice(0, 256), slice(256, 512))
-    ]
-    place(slice(512, 768), *halves)
+    )
+    stack[HALF:, :HALF] = jnp.where(swap, b, a).astype(BF16)
+    falling = jnp.where(swap, a, b).astype(BF16)
+    falling = jnp.dot(falling, flip[...], preferred_element_type=F32).astype(BF16)
+    stack[HALF:, HALF:] = falling
+    loads[1].wait()
 
     stores = []
     for part in range(4):
@@ -423,7 +446,7 @@
     own, got = pl.pallas_call(
         spectrum_kernel,
         out_shape=(
-            jax.ShapeDtypeStruct((SLOTS, WIN, GRID), F32),
+            jax.ShapeDtypeStruct((SLOTS, 2, WIN, GRID), BF16),
             jax.ShapeDtypeStruct((SLOTS, 2, WIN, HALF), BF16),
         ),
         in_specs=[hbm] * 3 + [vmem],
@@ -444,12 +467,15 @@
             pltpu.VMEM((QUARTER, 256), F32),
             pltpu.VMEM((TM, 2, 32, GRID), BF16),
             pltpu.VMEM((SLOTS, 2, WIN, HALF), BF16),
+            pltpu.VMEM((SLOTS, 2, WIN, GRID), BF16),
+            pltpu.VMEM((HALF, HALF), BF16),
             dma((SLOTS,)),
             dma((SLOTS,)),
             dma((SLOTS,)),
             dma((SLOTS, 2)),
             dma((SLOTS, 2)),
             dma((3,)),
+            dma((8,)),
             dma((SLOTS,)),
         ],
         compiler_params=pltpu.CompilerParams(
@@ -467,9 +493,8 @@
         in_specs=[hbm, hbm],
         out_specs=hbm,
         scratch_shapes=[
-            pltpu.VMEM((256, GRID), F32),
+            pltpu.VMEM((768, GRID), BF16),
             pltpu.VMEM((SLOTS, 2, WIN, HALF), BF16),
-            pltpu.VMEM((768, GRID), BF16),
             pltpu.VMEM((HALF, 768), BF16),
             pltpu.VMEM((HALF, HALF), BF16),
             pltpu.VMEM((4, WIN, 8, 256), F32),
@@ -477,7 +502,7 @@
             dma((4,)),
         ],
         compiler_params=pltpu.CompilerParams(vmem_limit_bytes=VMEM_ALL),
-    )(own.reshape(256, GRID), got)
+    )(own.reshape(HALF, GRID), got)
 
 
 def solution(mesh):

time: 80 us -> 79.2 us (0.990)
  no operation moved by 1% of the time
where the time goes in v4:
time: 79.2 us; the launch traced here: 78.2 us
  Pallas kernels  78.2 us (99%)
    pallas_call x1, Pallas kernels, body(): pl.pallas_call(spectrum_kernel, out_shape=(jax.ShapeDtypeStruct((SLOTS, 2...  74.7 us
    pallas_call x1, Pallas kernels, body(): pl.pallas_call(functools.partial(final_kernel, 1.0 / ((TM - 1) * energy))...  3.46 us

profile of v4, /device:TPU:69, one launch (start us, length us, event | category | flops | bytes accessed | tf_op | source)
XLA Modules:
  0.0 78.2 jit_solution(4995830959370582881)
XLA Ops:
  0.0 74.7 %shard_map.46 = (bf16[4,2,64,1024]{3,2,1,0:T(8,128)(2,1)}, bf16[4,2,64,512]{3,2,1,0:T(8,128)(2,1)}) custom-call(bf16[32,64,1024]{2,1,0:T(8,128)(2,1)} %h_hbm.1, bf16[4,256,512]{2,1,0:T(8,128)(2,1)} %constant.6.clone.ty_hbm, bf16[512,1024]{1,0:T(8,128)(2,1)} %constant.7.clone.tx_hbm, bf16[256,128]{1,0:T(8,128)(2,1)} %constant.8.clone.time_ref), custom_call_target="tpu_custom_call" | custom-call | tf_op jit(solution)/shard_map/pallas_call | solution.py:446
  74.7 3.5 %shard_map.47 = f32[64,8,1024]{2,1,0:T(8,128)} custom-call(bf16[512,1024]{1,0:T(8,128)(2,1)} %bitcast.1, bf16[4,2,64,512]{3,2,1,0:T(8,128)(2,1)} %get-tuple-element.8.got_hbm), custom_call_target="tpu_custom_call" | custom-call | tf_op jit(solution)/shard_map/pallas_call | solution.py:490

commit v5 on v4

--- a/solution.py
+++ b/solution.py
@@ -316,13 +316,9 @@
         swap = (lax.broadcasted_iota(jnp.int32, (WIN, HALF), 1) >= 1) & (me >= 64)
         a, b = own_ref[slot, :, :HALF], own_ref[slot, :, HALF:]
         a, b = jnp.where(swap, b, a), jnp.where(swap, a, b)
-        a_top, b_top = a.astype(BF16), b.astype(BF16)
-        stack[slot, 0, :, :HALF] = a_top
-        stack[slot, 1, :, :HALF] = (a - a_top.astype(F32)).astype(BF16)
-        falling = jnp.concatenate([b_top, (b - b_top.astype(F32)).astype(BF16)], 0)
-        falling = jnp.dot(falling, flip[...], preferred_element_type=F32).astype(BF16)
-        stack[slot, 0, :, HALF:] = falling[:WIN]
-        stack[slot, 1, :, HALF:] = falling[WIN:]
+        falling = jnp.dot(b.astype(BF16), flip[...], preferred_element_type=F32)
+        stack[slot, :, :HALF] = a.astype(BF16)
+        stack[slot, :, HALF:] = falling.astype(BF16)
 
     def own_copy(slot):
         return pltpu.make_async_copy(stack.at[slot], own_hbm.at[slot], own_sem.at[slot])
@@ -384,10 +380,14 @@
 def final_kernel(
     scale, own_hbm, got_hbm, out_hbm, stack, got_ref, left, flip, result, in_sem, out_sem
 ):
-    loads = [
-        pltpu.make_async_copy(got_hbm, got_ref, in_sem.at[0]),
-        pltpu.make_async_copy(own_hbm, stack.at[pl.ds(0, HALF)], in_sem.at[1]),
-    ]
+    loads = [pltpu.make_async_copy(got_hbm, got_ref, in_sem.at[0])]
+    for half in range(2):
+        columns = pl.ds(half * HALF, HALF)
+        loads.append(
+            pltpu.make_async_copy(
+                own_hbm.at[:, columns], stack.at[pl.ds(0, 256), columns], in_sem.at[1 + half]
+            )
+        )
     for load in loads:
         load.start()
     me = lax.axis_index("tm") * ROWS + lax.axis_index("rows")
@@ -396,36 +396,14 @@
     to = lax.broadcasted_iota(jnp.int32, (HALF, HALF), 0)
     come = lax.broadcasted_iota(jnp.int32, (HALF, HALF), 1)
     w, row = to // 8, to % 8
-    w_from = jnp.where(upper, (WIN - w) % WIN, w)
-    slot_own = jnp.where(
-        upper, jnp.where((row >= 1) & (row <= 4), 4 - row, -1), jnp.where(row < 4, row, -1)
-    )
-    slot_got = jnp.where(
-        upper,
-        jnp.where(row == 0, 0, jnp.where(row >= 5, 8 - row, -1)),
-        jnp.where(row >= 4, row - 4, -1),
-    )
-    from_own = (come // 128 == slot_own) & (come % WIN == w_from)
-    from_got = come == slot_got * WIN + w_from
-    left[:, :HALF] = jnp.where(from_own, 1.0, 0.0).astype(BF16)
-    left[:, HALF:] = jnp.where(from_got, 1.0, 0.0)[:, :256].astype(BF16)
+    mirrored = jnp.where(row == 0, 4, jnp.where(row <= 4, 4 - row, 12 - row))
+    source = jnp.where(upper, mirrored * WIN + (WIN - w) % WIN, row * WIN + w)
+    left[...] = jnp.where(come == source, 1.0, 0.0).astype(BF16)
     swap = (lax.broadcasted_iota(jnp.int32, (256, HALF), 1) >= 1) & upper
 
-    loads[0].wait()
-    a, b = (
-        jnp.concatenate(
-            [got_ref[:, part, :, at].reshape(256, 256).astype(F32) for part in range(2)], 1
-        )
-        for at in (slice(0, 256), slice(256, 512))
-    )
-    stack[HALF:, :HALF] = jnp.where(swap, b, a).astype(BF16)
-    falling = jnp.where(swap, a, b).astype(BF16)
-    falling = jnp.dot(falling, flip[...], preferred_element_type=F32).astype(BF16)
-    stack[HALF:, HALF:] = falling
-    loads[1].wait()
-
     stores = []
-    for part in range(4):
+
+    def place(part):
         columns = slice(part * 256, part * 256 + 256)
         product = jnp.dot(left[...], stack[:, columns], preferred_element_type=F32) * scale
         result[part] = product.reshape(WIN, 8, 256)
@@ -434,6 +412,24 @@
         )
         store.start()
         stores.append(store)
+
+    loads[0].wait()
+    a, b = (
+        jnp.concatenate(
+            [got_ref[:, part, :, at].reshape(256, 256).astype(F32) for part in range(2)], 1
+        )
+        for at in (slice(0, 256), slice(256, 512))
+    )
+    stack[256:, :HALF] = jnp.where(swap, b, a).astype(BF16)
+    loads[1].wait()
+    place(0)
+    place(1)
+    falling = jnp.where(swap, a, b).astype(BF16)
+    falling = jnp.dot(falling, flip[...], preferred_element_type=F32)
+    stack[256:, HALF:] = falling.astype(BF16)
+    loads[2].wait()
+    place(2)
+    place(3)
     for store in stores:
         store.wait()
 
@@ -446,7 +442,7 @@
     own, got = pl.pallas_call(
         spectrum_kernel,
         out_shape=(
-            jax.ShapeDtypeStruct((SLOTS, 2, WIN, GRID), BF16),
+            jax.ShapeDtypeStruct((SLOTS, WIN, GRID), BF16),
             jax.ShapeDtypeStruct((SLOTS, 2, WIN, HALF), BF16),
         ),
         in_specs=[hbm] * 3 + [vmem],
@@ -467,7 +463,7 @@
             pltpu.VMEM((QUARTER, 256), F32),
             pltpu.VMEM((TM, 2, 32, GRID), BF16),
             pltpu.VMEM((SLOTS, 2, WIN, HALF), BF16),
-            pltpu.VMEM((SLOTS, 2, WIN, GRID), BF16),
+            pltpu.VMEM((SLOTS, WIN, GRID), BF16),
             pltpu.VMEM((HALF, HALF), BF16),
             dma((SLOTS,)),
             dma((SLOTS,)),
@@ -493,16 +489,16 @@
         in_specs=[hbm, hbm],
         out_specs=hbm,
         scratch_shapes=[
-            pltpu.VMEM((768, GRID), BF16),
+            pltpu.VMEM((HALF, GRID), BF16),
             pltpu.VMEM((SLOTS, 2, WIN, HALF), BF16),
-            pltpu.VMEM((HALF, 768), BF16),
+            pltpu.VMEM((HALF, HALF), BF16),
             pltpu.VMEM((HALF, HALF), BF16),
             pltpu.VMEM((4, WIN, 8, 256), F32),
-            dma((2,)),
+            dma((3,)),
             dma((4,)),
         ],
         compiler_params=pltpu.CompilerParams(vmem_limit_bytes=VMEM_ALL),
-    )(own.reshape(HALF, GRID), got)
+    )(own.reshape(256, GRID), got)
 
 
 def solution(mesh):

time: 79.2 us -> 78.9 us (level)
  no operation moved by 1% of the time
where the time goes in v5:
time: 78.9 us; the launch traced here: 78 us
  Pallas kernels  77.9 us (99%)
    pallas_call x1, Pallas kernels, body(): pl.pallas_call(spectrum_kernel, out_shape=(jax.ShapeDtypeStruct((SLOTS, W...  74.7 us
    pallas_call x1, Pallas kernels, body(): pl.pallas_call(functools.partial(final_kernel, 1.0 / ((TM - 1) * energy))...  3.23 us

profile of v5, /device:TPU:69, one launch (start us, length us, event | category | flops | bytes accessed | tf_op | source)
XLA Modules:
  0.0 78.0 jit_solution(3173865288457170632)
XLA Ops:
  0.0 74.7 %shard_map.46 = (bf16[4,64,1024]{2,1,0:T(8,128)(2,1)}, bf16[4,2,64,512]{3,2,1,0:T(8,128)(2,1)}) custom-call(bf16[32,64,1024]{2,1,0:T(8,128)(2,1)} %h_hbm.1, bf16[4,256,512]{2,1,0:T(8,128)(2,1)} %constant.6.clone.ty_hbm, bf16[512,1024]{1,0:T(8,128)(2,1)} %constant.7.clone.tx_hbm, bf16[256,128]{1,0:T(8,128)(2,1)} %constant.8.clone.time_ref), custom_call_target="tpu_custom_call" | custom-call | tf_op jit(solution)/shard_map/pallas_call | solution.py:442
  74.7 3.2 %shard_map.47 = f32[64,8,1024]{2,1,0:T(8,128)} custom-call(bf16[256,1024]{1,0:T(8,128)(2,1)} %bitcast.1, bf16[4,2,64,512]{3,2,1,0:T(8,128)(2,1)} %get-tuple-element.8.got_hbm), custom_call_target="tpu_custom_call" | custom-call | tf_op jit(solution)/shard_map/pallas_call | solution.py:486

commit v6 on v5

--- a/solution.py
+++ b/solution.py
@@ -341,13 +341,16 @@
     row_tables(0)
     row_phase(0)
     pl.semaphore_wait(barrier, DEVICES - 1)
-    loads[1].wait()
-    for slot in range(1, SLOTS):
-        row_tables(slot)
 
     @pl.loop(0, SLOTS)
     def _(slot):
         start_sends(slot)
+
+        @pl.when(slot == 0)
+        def _():
+            loads[1].wait()
+            for other in range(1, SLOTS):
+                row_tables(other)
 
         @pl.when(slot < SLOTS - 1)
         def _():

time: 78.9 us -> 77.9 us (0.987)
  no operation moved by 1% of the time
where the time goes in v6:
time: 77.9 us; the launch traced here: 77.7 us
  Pallas kernels  77.7 us (100%)
    pallas_call x1, Pallas kernels, body(): pl.pallas_call(spectrum_kernel, out_shape=(jax.ShapeDtypeStruct((SLOTS, W...  74.4 us
    pallas_call x1, Pallas kernels, body(): pl.pallas_call(functools.partial(final_kernel, 1.0 / ((TM - 1) * energy))...  3.23 us

profile of v6, /device:TPU:69, one launch (start us, length us, event | category | flops | bytes accessed | tf_op | source)
XLA Modules:
  0.0 77.7 jit_solution(13375506091715822381)
XLA Ops:
  0.0 74.4 %shard_map.46 = (bf16[4,64,1024]{2,1,0:T(8,128)(2,1)}, bf16[4,2,64,512]{3,2,1,0:T(8,128)(2,1)}) custom-call(bf16[32,64,1024]{2,1,0:T(8,128)(2,1)} %h_hbm.1, bf16[4,256,512]{2,1,0:T(8,128)(2,1)} %constant.6.clone.ty_hbm, bf16[512,1024]{1,0:T(8,128)(2,1)} %constant.7.clone.tx_hbm, bf16[256,128]{1,0:T(8,128)(2,1)} %constant.8.clone.time_ref), custom_call_target="tpu_custom_call" | custom-call | tf_op jit(solution)/shard_map/pallas_call | solution.py:445
  74.5 3.2 %shard_map.47 = f32[64,8,1024]{2,1,0:T(8,128)} custom-call(bf16[256,1024]{1,0:T(8,128)(2,1)} %bitcast.1, bf16[4,2,64,512]{3,2,1,0:T(8,128)(2,1)} %get-tuple-element.8.got_hbm), custom_call_target="tpu_custom_call" | custom-call | tf_op jit(solution)/shard_map/pallas_call | solution.py:489

commit v7 on v6

--- a/solution.py
+++ b/solution.py
@@ -200,7 +200,7 @@
             x_of = [(x + 3 * turn + d) % 4 * 2 for d in range(4)]
 
             def start(step):
-                shift = step * 91 % DEVICES
+                shift = step * 107 % DEVICES
                 to_tm = x_of[shift // 32] + z_tm[shift // 2 % 4]
                 to_rows = z_rows[shift // 2 % 4] + y_of[shift // 8 % 4] + core_of[shift % 2]
                 target = to_tm * ROWS + to_rows

time: 77.9 us -> 76.1 us (0.977)
  the two profiles are of different devices: /device:TPU:69 before, /device:TPU:1 now
where the time goes in v7:
time: 76.1 us; the launch traced here: 76 us
  Pallas kernels  76 us (100%)
    pallas_call x1, Pallas kernels, body(): pl.pallas_call(spectrum_kernel, out_shape=(jax.ShapeDtypeStruct((SLOTS, W...  72.7 us
    pallas_call x1, Pallas kernels, body(): pl.pallas_call(functools.partial(final_kernel, 1.0 / ((TM - 1) * energy))...  3.23 us

profile of v7, /device:TPU:1, one launch (start us, length us, event | category | flops | bytes accessed | tf_op | source)
XLA Modules:
  0.0 76.0 jit_solution(4526244915326853767)
XLA Ops:
  0.0 72.7 %shard_map.46 = (bf16[4,64,1024]{2,1,0:T(8,128)(2,1)}, bf16[4,2,64,512]{3,2,1,0:T(8,128)(2,1)}) custom-call(bf16[32,64,1024]{2,1,0:T(8,128)(2,1)} %h_hbm.1, bf16[4,256,512]{2,1,0:T(8,128)(2,1)} %constant.6.clone.ty_hbm, bf16[512,1024]{1,0:T(8,128)(2,1)} %constant.7.clone.tx_hbm, bf16[256,128]{1,0:T(8,128)(2,1)} %constant.8.clone.time_ref), custom_call_target="tpu_custom_call" | custom-call | tf_op jit(solution)/shard_map/pallas_call | solution.py:445
  72.7 3.2 %shard_map.47 = f32[64,8,1024]{2,1,0:T(8,128)} custom-call(bf16[256,1024]{1,0:T(8,128)(2,1)} %bitcast.1, bf16[4,2,64,512]{3,2,1,0:T(8,128)(2,1)} %get-tuple-element.8.got_hbm), custom_call_target="tpu_custom_call" | custom-call | tf_op jit(solution)/shard_map/pallas_call | solution.py:489

commit v8 on v7

--- a/solution.py
+++ b/solution.py
@@ -200,7 +200,7 @@
             x_of = [(x + 3 * turn + d) % 4 * 2 for d in range(4)]
 
             def start(step):
-                shift = step * 107 % DEVICES
+                shift = step * 11 % DEVICES
                 to_tm = x_of[shift // 32] + z_tm[shift // 2 % 4]
                 to_rows = z_rows[shift // 2 % 4] + y_of[shift // 8 % 4] + core_of[shift % 2]
                 target = to_tm * ROWS + to_rows

time: 76.1 us -> 76.1 us (level)
  no operation moved by 1% of the time
where the time goes in v8:
time: 76.1 us; the launch traced here: 75.9 us
  Pallas kernels  75.9 us (100%)
    pallas_call x1, Pallas kernels, body(): pl.pallas_call(spectrum_kernel, out_shape=(jax.ShapeDtypeStruct((SLOTS, W...  72.7 us
    pallas_call x1, Pallas kernels, body(): pl.pallas_call(functools.partial(final_kernel, 1.0 / ((TM - 1) * energy))...  3.23 us

profile of v8, /device:TPU:1, one launch (start us, length us, event | category | flops | bytes accessed | tf_op | source)
XLA Modules:
  0.0 75.9 jit_solution(18135577713859520411)
XLA Ops:
  0.0 72.7 %shard_map.46 = (bf16[4,64,1024]{2,1,0:T(8,128)(2,1)}, bf16[4,2,64,512]{3,2,1,0:T(8,128)(2,1)}) custom-call(bf16[32,64,1024]{2,1,0:T(8,128)(2,1)} %h_hbm.1, bf16[4,256,512]{2,1,0:T(8,128)(2,1)} %constant.6.clone.ty_hbm, bf16[512,1024]{1,0:T(8,128)(2,1)} %constant.7.clone.tx_hbm, bf16[256,128]{1,0:T(8,128)(2,1)} %constant.8.clone.time_ref), custom_call_target="tpu_custom_call" | custom-call | tf_op jit(solution)/shard_map/pallas_call | solution.py:445
  72.7 3.2 %shard_map.47 = f32[64,8,1024]{2,1,0:T(8,128)} custom-call(bf16[256,1024]{1,0:T(8,128)(2,1)} %bitcast.1, bf16[4,2,64,512]{3,2,1,0:T(8,128)(2,1)} %get-tuple-element.8.got_hbm), custom_call_target="tpu_custom_call" | custom-call | tf_op jit(solution)/shard_map/pallas_call | solution.py:489
